TPU v7x, 256 devices: a whole 4x4x8 slice. The times are simulated.
256 devices in a mesh: pix: 32 (over y, x, core), site: 8 (over z).
Axes of the slice: x: 4, y: 4, z: 8, core: 2. Of those that a mesh axis runs over, the one named last changes fastest.
Arguments:
- margins: int32 [2048, 256, 1024], P('pix', None, 'site'), may hold values from -2047 to 2047
- block_pos: int32 [2048, 8], P('pix', 'site'), may hold values from -1 to 15, as said below
- pattern_ids: int32 [1024], P('site'), may hold values from 0 to 15
- pattern_gain: float32 [16, 256], replicated, may hold values from -4 to 4
- site_price: float32 [1024], P('site'), may hold values from 0.2 to 4
- weights: float32 [131072], P('pix'), may hold values from 0.2 to 2
- site_start: float32 [1024], P('site'), may hold values from 0 to 1
- pixel_start: float32 [131072], P('pix'), may hold values from 0 to 1
- dual_start: float32 [131072], P('pix'), may hold values from 0 to 2
Outputs:
- site_level: float32 [1024], P('site')
- pixel_level: float32 [131072], P('pix')
- duals: float32 [131072], P('pix')
Inputs may be any that keep to these rules, and one draw needn't show every extreme that they name: Row k of block_pos and of margins is held by pixel device k // 64 and belongs to pixel device (k // 2) % 32; its entry for site block b is the position, among that device's 16 pixel blocks, of the pixel block of the tile, or -1 for an empty slot. The lists are filled unevenly. For one pixel device, drawn afresh, every slot that belongs to it is filled in every row group and site block.
All inputs are finite; a program needn't handle non-finite values.
Results may differ from a plain program's by a relative error of at most 0.0003.
Values may be sent and summed in bfloat16 or wider, within the bound.
No kernel may reach another device: no remote copies, remote signals or barrier semaphores. Data moves between devices by JAX's collectives and lax.ppermute only.
A program may use at most 64 MiB of HBM per device.

v0:
```python
import jax
import jax.numpy as jnp
from jax import lax
from jax.sharding import PartitionSpec as P

ITERS = 2


MARGIN_SCALE = 2.0 ** (-9)


def build_tiles(margins, block_pos, pattern_ids, pattern_gain):
    patterns = pattern_gain.shape[0]
    chooser = (pattern_ids[:, None] == jnp.arange(patterns, dtype=jnp.int32)[None, :]).astype(
        jnp.float32
    )
    gain_tile = lax.dot_general(
        pattern_gain, chooser, (((0,), (1,)), ((), ())), precision=lax.Precision.HIGHEST
    )
    filled = block_pos[:, 0] >= 0
    values = jax.nn.sigmoid(margins.astype(jnp.float32) * MARGIN_SCALE + gain_tile[None])
    return jnp.where(filled[:, None, None], values, 0.0).astype(jnp.bfloat16)


def local(
    margins,
    block_pos,
    pattern_ids,
    pattern_gain,
    site_price,
    weights,
    site_start,
    pixel_start,
    dual_start,
):
    slot_count = margins.shape[0]
    block_width = pattern_gain.shape[1]
    blocks = weights.shape[0] // block_width
    coverage = build_tiles(margins, block_pos, pattern_ids, pattern_gain)
    position = block_pos[:, 0]
    tiles_here, arrived = (
        lax.all_to_all(coverage, "pix", split_axis=0, concat_axis=0, tiled=True),
        lax.all_to_all(
            position.astype(jnp.bfloat16), "pix", split_axis=0, concat_axis=0, tiled=True
        ),
    )
    chooser = arrived.astype(jnp.float32)[:, None] == jnp.arange(blocks, dtype=jnp.float32)[None, :]
    chooser_half = chooser.astype(jnp.bfloat16)
    chooser_full = chooser.astype(jnp.float32)

    def spread_rows(products):
        return jnp.einsum("kb,tkr->btr", chooser_full, products, precision=lax.Precision.HIGHEST)

    def column_totals(selected):
        partial_value = jnp.einsum(
            "tkr,krj->tj", selected, tiles_here, preferred_element_type=jnp.float32
        )
        return lax.psum(partial_value, "pix")

    def row_totals(values):
        products = jnp.einsum("krj,tj->tkr", tiles_here, values, preferred_element_type=jnp.float32)
        return lax.psum(spread_rows(products), "site")

    ones_pixels = jnp.ones((1, slot_count, block_width), jnp.bfloat16)
    ones_sites = jnp.ones((1, tiles_here.shape[2]), jnp.bfloat16)
    column_sum = column_totals(ones_pixels)[0]
    row_sum = row_totals(ones_sites)[:, 0, :].reshape(-1)
    site_level, pixel_level, duals = (site_start, pixel_start, dual_start)
    for iteration in range(ITERS):
        dual_half = duals.astype(jnp.bfloat16).reshape(blocks, block_width)
        selected = jnp.dot(chooser_half, dual_half, preferred_element_type=jnp.float32).astype(
            jnp.bfloat16
        )[None]
        pulled = column_totals(selected)[0]
        new_site = jnp.clip(site_level - (site_price - pulled / column_sum), 0.0, 1.0)
        new_pixel = jnp.clip(pixel_level - (duals - weights), 0.0, 1.0)
        extrapolated = (2.0 * new_site - site_level).astype(jnp.bfloat16)[None]
        pushed = row_totals(extrapolated)[:, 0, :].reshape(-1)
        duals = jnp.maximum(duals + (2.0 * new_pixel - pixel_level - pushed) / (row_sum + 1.0), 0.0)
        site_level, pixel_level = (new_site, new_pixel)
    return (site_level, pixel_level, duals)


def solution(mesh):
    placed = (
        P("pix", None, "site"),
        P("pix", "site"),
        P("site"),
        P(),
        P("site"),
        P("pix"),
        P("site"),
        P("pix"),
        P("pix"),
    )
    return jax.shard_map(
        local,
        mesh=mesh,
        in_specs=placed,
        out_specs=(P("site"), P("pix"), P("pix")),
        check_vma=False,
    )
```

profile of v0, /device:TPU:1, one launch (start us, length us, event | category | flops | bytes accessed | tf_op | source)
XLA Modules:
  0.0 279.4 jit_solution(2345974059912617424)
XLA Ops:
  0.6 0.0 copy-start
  0.6 0.7 convert_reduce_fusion.1
  1.3 0.7 convert_element_type.63
  2.1 8.6 %all-to-all-start = ((bf16[32,2,1]{1,2,0:T(2,128)(2,1)}), bf16[32,2,1]{1,2,0:T(2,128)(2,1)S(1)}, u32[]{:S(2)}, u32[]{:S(2)}) async-start(bf16[32,2,1]{1,2,0:T(2,128)(2,1)} %convert_element_type.63), calls=%async_computation | async-start | bytes 32768 | tf_op jit(solution)/shard_map/all_to_all | solution.py:43
  10.6 0.7 compare_bitcast_fusion
  11.3 0.0 copy-done
  11.3 0.9 convolution_bitcast_fusion
  12.2 0.1 copy.15
  12.3 6.3 %select_convert_fusion = bf16[64,256,128]{2,1,0:T(8,128)(2,1)} fusion(s32[64,256,128]{2,1,0:T(8,128)} %param.9, f32[256,128]{1,0:T(8,128)S(1)} %copy.15, pred[64]{0:T(512)(128)(4,1)S(1)} %compare_bitcast_fusion), kind=kLoop, calls=%fused_computation | loop fusion | flops 16777216 | bytes 12714048 | tf_op jit(solution)/shard_map/convert_element_type | solution.py:22
  18.6 0.0 copy-start.1
  18.6 0.0 all-to-all-done
  18.6 7.6 %all-to-all-start.1 = ((bf16[64,256,128]{2,1,0:T(8,128)(2,1)}), bf16[64,256,128]{2,1,0:T(8,128)(2,1)}, u32[]{:S(2)}, u32[]{:S(2)}) async-start(bf16[64,256,128]{2,1,0:T(8,128)(2,1)} %select_convert_fusion), calls=%async_computation.1 | async-start | bytes 8388608 | tf_op jit(solution)/shard_map/all_to_all | solution.py:42
  26.2 0.0 copy-done.1
  26.2 0.1 convert_reduce_fusion
  26.3 0.1 reshape.74
  26.4 0.2 fusion
  26.6 0.0 copy-start.4
  26.6 0.0 copy-start.6
  26.6 50.3 %all-to-all-done.1 = bf16[64,256,128]{2,1,0:T(8,128)(2,1)} async-done(((bf16[64,256,128]{2,1,0:T(8,128)(2,1)}), bf16[64,256,128]{2,1,0:T(8,128)(2,1)}, u32[]{:S(2)}, u32[]{:S(2)}) %all-to-all-start.1) | async-done | bytes 4194336 | tf_op jit(solution)/shard_map/all_to_all | solution.py:42
  76.8 2.8 %convolution_bitcast_fusion.5 = f32[1,128]{1,0:T(1,128)S(1)} fusion(bf16[64,256,128]{2,1,0:T(8,128)(2,1)} %all-to-all-done.1), kind=kOutput, calls=%fused_computation.10 | convolution fusion | flops 4194304 | bytes 4194816 | tf_op jit(solution)/shard_map/tkr,krj->tj/dot_general | solution.py:55
  79.7 2.9 %convolution_bitcast_fusion.6 = f32[1,128]{1,0:T(1,128)S(1)} fusion(bf16[64,256,128]{2,1,0:T(8,128)(2,1)} %all-to-all-done.1, bf16[64,256,1]{1,0,2:T(8,128)(2,1)S(1)} %fusion), kind=kOutput, calls=%fused_computation.11 | convolution fusion | flops 4194304 | bytes 4227584 | tf_op jit(solution)/shard_map/tkr,krj->tj/dot_general | solution.py:55
  82.6 65.6 %all-reduce = (f32[1,128]{1,0:T(1,128)S(1)}, f32[1,128]{1,0:T(1,128)S(1)}) all-reduce(f32[1,128]{1,0:T(1,128)S(1)} %convolution_bitcast_fusion.6, f32[1,128]{1,0:T(1,128)S(1)} %convolution_bitcast_fusion.5), channel_id=1, replica_groups=mesh['pix'=32,'site'=8] {'pix'}, use_global_device_ids=true, to_apply=%region_0.1 | all-reduce | flops 256 | bytes 2048 | tf_op jit(solution)/shard_map/psum | solution.py:58
  148.2 0.0 copy-done.4
  148.2 0.0 copy-done.6
  148.2 0.0 copy-start.2
  148.2 0.0 copy-start.3
  148.3 3.4 %fusion.21 = f32[1,64,256]{2,0,1:T(1,128)S(1)} fusion(bf16[64,256,128]{2,1,0:T(8,128)(2,1)} %all-to-all-done.1, f32[128]{0:T(128)S(1)} %copy-done.4, f32[128]{0:T(128)S(1)} %fusion.24), kind=kOutput, calls=%fused_computation.41 | convolution fusion | flops 4194688 | bytes 4260864 | tf_op jit(solution)/shard_map/krj,tj->tkr/dot_general | solution.py:61
  151.6 0.3 convolution_bitcast_fusion.3
  151.9 3.4 %fusion.31 = f32[1,64,256]{2,0,1:T(1,128)S(1)} fusion(bf16[64,256,128]{2,1,0:T(8,128)(2,1)} %all-to-all-done.1), kind=kOutput, calls=%fused_computation.53 | convolution fusion | flops 4194304 | bytes 4259840 | tf_op jit(solution)/shard_map/krj,tj->tkr/dot_general | solution.py:61
  155.3 0.3 convolution_bitcast_fusion.2
  155.6 25.5 %all-reduce.1 = (f32[16,1,256]{2,0,1:T(8,128)S(1)}, f32[4096]{0:T(1024)S(1)}) all-reduce(f32[16,1,256]{2,0,1:T(8,128)S(1)} %convolution_bitcast_fusion.2, f32[4096]{0:T(1024)S(1)} %bitcast.70), channel_id=1, replica_groups=mesh['pix'=32,'site'=8] {'site'}, use_global_device_ids=true, to_apply=%region_3.4 | all-reduce | flops 8192 | bytes 65536 | tf_op jit(solution)/shard_map/psum | solution.py:62
  181.1 0.0 copy-done.2
  181.1 0.0 copy-done.3
  181.2 0.2 fusion.1
  181.4 2.9 %convolution_bitcast_fusion.4 = f32[1,128]{1,0:T(1,128)S(1)} fusion(bf16[64,256,128]{2,1,0:T(8,128)(2,1)} %all-to-all-done.1, bf16[64,256,1]{1,0,2:T(8,128)(2,1)S(1)} %fusion.1), kind=kOutput, calls=%fused_computation.9 | convolution fusion | flops 4194304 | bytes 4227584 | tf_op jit(solution)/shard_map/tkr,krj->tj/dot_general | solution.py:55
  184.3 70.5 %psum.46 = f32[1,128]{1,0:T(1,128)S(1)} all-reduce(f32[1,128]{1,0:T(1,128)S(1)} %convolution_bitcast_fusion.4), channel_id=1, replica_groups=mesh['pix'=32,'site'=8] {'pix'}, use_global_device_ids=true, to_apply=%region_4.5 | all-reduce | flops 128 | bytes 1024 | tf_op jit(solution)/shard_map/psum | solution.py:58
  254.8 0.0 copy-start.5
  254.8 3.4 %fusion.17 = f32[1,64,256]{2,0,1:T(1,128)S(1)} fusion(bf16[64,256,128]{2,1,0:T(8,128)(2,1)} %all-to-all-done.1, f32[128]{0:T(128)S(1)} %fusion.24, f32[128]{0:T(128)S(1)} %fusion.20), kind=kOutput, calls=%fused_computation.36 | convolution fusion | flops 4194688 | bytes 4260864 | tf_op jit(solution)/shard_map/krj,tj->tkr/dot_general | solution.py:61
  258.1 0.3 convolution_bitcast_fusion.1
  258.4 20.4 %psum.47 = f32[4096]{0:T(1024)S(1)} all-reduce(f32[4096]{0:T(1024)S(1)} %bitcast.71), channel_id=1, replica_groups=mesh['pix'=32,'site'=8] {'site'}, use_global_device_ids=true, to_apply=%region_5.6 | all-reduce | flops 4096 | bytes 32768 | tf_op jit(solution)/shard_map/psum | solution.py:62
  278.8 0.6 add_maximum_fusion
  279.4 0.0 copy-done.5
  (10 shorter events, 0.1 us)
Async XLA Ops:
  0.6 10.7 %copy-start = (f32[16,256]{1,0:T(8,128)S(1)}, f32[16,256]{1,0:T(8,128)}, u32[]{:S(2)}) copy-start(f32[16,256]{1,0:T(8,128)} %param.12) | copy-start | bytes 49156
  2.1 16.5 %all-to-all-start = ((bf16[32,2,1]{1,2,0:T(2,128)(2,1)}), bf16[32,2,1]{1,2,0:T(2,128)(2,1)S(1)}, u32[]{:S(2)}, u32[]{:S(2)}) async-start(bf16[32,2,1]{1,2,0:T(2,128)(2,1)} %convert_element_type.63), calls=%async_computation | async-start | bytes 32768 | tf_op jit(solution)/shard_map/all_to_all | solution.py:43
  18.6 7.6 %copy-start.1 = (f32[4096]{0:T(1024)S(1)}, f32[4096]{0:T(1024)}, u32[]{:S(2)}) copy-start(f32[4096]{0:T(1024)} %param.17) | copy-start | bytes 49156
  18.6 58.3 %all-to-all-start.1 = ((bf16[64,256,128]{2,1,0:T(8,128)(2,1)}), bf16[64,256,128]{2,1,0:T(8,128)(2,1)}, u32[]{:S(2)}, u32[]{:S(2)}) async-start(bf16[64,256,128]{2,1,0:T(8,128)(2,1)} %select_convert_fusion), calls=%async_computation.1 | async-start | bytes 8388608 | tf_op jit(solution)/shard_map/all_to_all | solution.py:42
  26.6 121.7 %copy-start.4 = (f32[128]{0:T(128)S(1)}, f32[128]{0:T(128)}, u32[]{:S(2)}) copy-start(f32[128]{0:T(128)} %param.15) | copy-start | bytes 1540
  26.6 121.7 %copy-start.6 = (f32[128]{0:T(128)S(1)}, f32[128]{0:T(128)}, u32[]{:S(2)}) copy-start(f32[128]{0:T(128)} %param.13) | copy-start | bytes 1540
  148.2 32.9 %copy-start.2 = (f32[4096]{0:T(1024)S(1)}, f32[4096]{0:T(1024)}, u32[]{:S(2)}) copy-start(f32[4096]{0:T(1024)} %param.16) | copy-start | bytes 49156
  148.2 32.9 %copy-start.3 = (f32[4096]{0:T(1024)S(1)}, f32[4096]{0:T(1024)}, u32[]{:S(2)}) copy-start(f32[4096]{0:T(1024)} %param.14) | copy-start | bytes 49156
  254.8 24.7 %copy-start.5 = (f32[128]{0:T(128)}, f32[128]{0:T(128)S(1)}, u32[]{:S(2)}) copy-start(f32[128]{0:T(128)S(1)} %fusion.20) | copy-start | bytes 1540
where the time goes:
time: 285 us; the launch traced here: 279 us
  blocking collectives  182 us (64%)
  waiting for transfers between devices  50.3 us (18%)
  matrix products  20.9 us (7%)
  starting transfers between devices  16.1 us (6%)
  other arithmetic  8.33 us (3%)
    psum x2, blocking collectives, column_totals(): return lax.psum(partial_value, 'pix')  136 us
    all_to_all x1, waiting for transfers between devices, local(): lax.all_to_all(coverage, 'pix', split_axis=0, concat_axis=0, tiled=True)  50.3 us
    psum x2, blocking collectives, row_totals(): return lax.psum(spread_rows(products), 'site')  45.9 us
    dot_general x3, matrix products, row_totals(): jnp.einsum('krj,tj->tkr', tiles_here, values, preferred_element_type=jnp....  10.1 us
    dot_general x3, matrix products, column_totals(): jnp.einsum('tkr,krj->tj', selected, tiles_here, preferred_element_type=jn...  8.67 us
    all_to_all x1, starting transfers between devices, local(): lax.all_to_all(position.astype(jnp.bfloat16), 'pix', split_axis=0, concat...  8.58 us
    all_to_all x1, starting transfers between devices, local(): lax.all_to_all(coverage, 'pix', split_axis=0, concat_axis=0, tiled=True)  7.56 us
    convert_element_type x1, other arithmetic, build_tiles(): return jnp.where(filled[:, None, None], values, 0.0).astype(jnp.bfloat16)  6.26 us
  transfers between devices with their start and end apart: 2, of which 1 were waited for; matrix products, arithmetic and copies ran while one was open for 3% of the time, Pallas kernels for 0%

commit v1 on v0

v1 whole, which is shorter than its diff:
```python
import functools

import jax
import jax.numpy as jnp
from jax import lax
from jax.experimental import pallas as pl
from jax.experimental.pallas import tpu as pltpu
from jax.sharding import PartitionSpec as P

F32 = jnp.float32
BF16 = jnp.bfloat16
HALF_SCALE = 2.0 ** (-10)
VMEM = pl.BlockSpec(memory_space=pltpu.VMEM)


def iota(shape, dim):
    return lax.broadcasted_iota(jnp.int32, shape, dim)


def dot(a, b, dims=((1,), (0,))):
    return lax.dot_general(a, b, (dims, ((), ())), preferred_element_type=F32)


def exact_pick(onehot, values, dims):
    high = values.astype(BF16)
    rest = values - high.astype(F32)
    middle = rest.astype(BF16)
    low = (rest - middle.astype(F32)).astype(BF16)
    return dot(onehot, high, dims) + (dot(onehot, middle, dims) + dot(onehot, low, dims))


def call(body, outs, *args, scratch=(), specs=None, flops=0, nbytes=0):
    return pl.pallas_call(
        body,
        out_shape=[jax.ShapeDtypeStruct(s, d) for s, d in outs],
        in_specs=specs or [VMEM] * len(args),
        out_specs=[VMEM] * len(outs),
        scratch_shapes=list(scratch),
        cost_estimate=pl.CostEstimate(flops=flops, transcendentals=0, bytes_accessed=nbytes),
        compiler_params=pltpu.CompilerParams(vmem_limit_bytes=48 * 1024 * 1024),
    )(*args)


def build_kernel(chunks, m_hbm, pos_ref, ids_ref, gain_ref, cov_ref, sum_ref, map_ref, buf, half_gain, sems):
    slots = m_hbm.shape[0]
    per = slots // chunks
    copies = []
    for c in range(chunks):
        part = pl.ds(c * per, per)
        copy = pltpu.make_async_copy(m_hbm.at[part], buf.at[part], sems.at[c])
        copy.start()
        copies.append(copy)
    patterns = gain_ref.shape[0]
    onehot = (ids_ref[...] == iota((patterns, 128), 0)).astype(BF16)
    half_gain[...] = 0.5 * gain_pick(gain_ref[...], onehot)
    rows = 4 * slots
    expand = (iota((rows, slots), 1) == (iota((rows, slots), 0) >> 2)).astype(BF16)
    wide = jnp.broadcast_to(pos_ref[...].astype(F32), (slots, 128)).astype(BF16)
    map_ref[...] = dot(expand, wide)
    sum_ref[...] = jnp.zeros_like(sum_ref)
    for c in range(chunks):
        copies[c].wait()

        def pair(t, carry):
            marks = map_ref[pl.ds(pl.multiple_of(t * 8, 8), 8), :]
            total = jnp.zeros((8, 128), F32)
            for i in range(2):
                level = buf[2 * t + i].astype(F32) * HALF_SCALE + half_gain[...]
                tile = (0.5 * jnp.tanh(level) + 0.5).astype(BF16)
                cov_ref[t, :, i * 128 : (i + 1) * 128] = tile
                part = jnp.sum(tile.astype(F32).reshape(-1, 8, 128), axis=0)
                total = total + jnp.where(marks[4 * i : 4 * i + 1] >= 0.0, part, 0.0)
            sum_ref[...] += total
            return carry

        lax.fori_loop(c * per // 2, (c + 1) * per // 2, pair, 0)


def gain_pick(gain, onehot):
    dims = ((0,), (0,))
    high = gain.astype(BF16)
    rest = gain - high.astype(F32)
    middle = rest.astype(BF16)
    low = (rest - middle.astype(F32)).astype(BF16)
    return dot(high, onehot, dims) + (dot(middle, onehot, dims) + dot(low, onehot, dims))


def pull(x_ref, cov_ref):
    first = (iota((8, 128), 0) & 2) == 0
    total = jnp.zeros((8, 256), F32)
    for t in range(cov_ref.shape[0]):
        x = x_ref[t * 8 : (t + 1) * 8, :]
        left = jnp.concatenate([jnp.where(first, x, 0.0), jnp.where(first, 0.0, x)], axis=1)
        total = total + dot(left.astype(BF16), cov_ref[t])
    own = jnp.where(iota((8, 128), 0) < 4, total[:, :128], total[:, 128:])
    return jnp.sum(own, axis=0, keepdims=True)


def push(row, plain, cov_ref, out_ref):
    spot = iota((8, 128), 0)
    value = jnp.broadcast_to(row, (8, 128))
    if plain:
        value = jnp.where((spot & 1) == 1, value, 1.0)
    left = jnp.concatenate([jnp.where(spot < 4, value, 0.0), jnp.where(spot < 4, 0.0, value)], axis=1).astype(BF16)
    first = (spot & 2) == 0
    for t in range(cov_ref.shape[0]):
        product = dot(left, cov_ref[t], ((1,), (1,)))
        out_ref[t * 8 : (t + 1) * 8, :] = jnp.where(first, product[:, :128], product[:, 128:])


def positions(marks):
    tiles = marks.reshape(-1, 8, 128)
    spot = iota(tiles.shape, 1)
    return jnp.where(spot < 2, tiles[:, 2:3, :], tiles).reshape(marks.shape)


def kinds(rows):
    spot = iota((rows, 128), 0)
    return (spot & 1).astype(F32), ((spot >> 1) & 1).astype(F32)


def first_pull_kernel(ag_ref, map_ref, cov_ref, sum_ref, out_ref, x_ref):
    rows = map_ref.shape[0]
    marks = map_ref[...]
    q, h = kinds(rows)
    tile = (iota((rows, 128), 0) >> 3).astype(F32)
    key = jnp.where((marks >= 0.0) & (q == 0.0), tile * 32.0 + marks * 2.0 + h, -1.0)
    picked = jnp.zeros((rows, 128), F32)
    for c in range(ag_ref.shape[0] // 128):
        lane = (iota((rows, 128), 1) + c * 128).astype(F32)
        picked = picked + dot((lane == key).astype(BF16), ag_ref[c * 128 : (c + 1) * 128, :])
    x_ref[...] = picked
    pulled = pull(x_ref, cov_ref)
    sums = jnp.sum(sum_ref[...], axis=0, keepdims=True)
    tiles = marks.reshape(-1, 8, 128)
    spot = iota(tiles.shape, 1)
    out_ref[...] = jnp.where(spot == 0, sums[None], jnp.where(spot == 1, pulled[None], tiles)).reshape(rows, 128)


def first_push_kernel(in_ref, price_ref, site_ref, cov_ref, out_ref, new_ref, sum_ref):
    totals = jnp.sum(in_ref[...].reshape(-1, 8, 128), axis=0)
    column_sum = totals[0:1]
    new = jnp.clip(site_ref[...] - (price_ref[...] - totals[1:2] / column_sum), 0.0, 1.0)
    new_ref[...] = new
    sum_ref[...] = column_sum
    push(2.0 * new - site_ref[...], True, cov_ref, out_ref)


def first_spread_kernel(x_ref, marks_ref, out_ref):
    rows = x_ref.shape[0]
    marks = positions(marks_ref[...])
    q, h = kinds(rows)
    key = jnp.where(marks >= 0.0, q * 32.0 + marks * 2.0 + h, -1.0)
    onehot = (iota((rows, 128), 1).astype(F32) == key).astype(BF16)[:, :64]
    spread = exact_pick(onehot, x_ref[...], ((0,), (0,)))
    for s in range(out_ref.shape[0]):
        out_ref[s] = spread


def step(pixel, dual, weight, pushed, row_sum):
    new = jnp.clip(pixel - (dual - weight), 0.0, 1.0)
    return new, jnp.maximum(dual + ((2.0 * new - pixel) - pushed) / (row_sum + 1.0), 0.0)


def first_dual_kernel(in_ref, marks_ref, dual_ref, weight_ref, pixel_ref, out_ref, new_dual_ref, new_pixel_ref, row_ref):
    totals = jnp.sum(in_ref[...], axis=0)
    row_sum = totals[:32]
    row_ref[...] = row_sum
    new_pixel, new_dual = step(pixel_ref[...], dual_ref[...], weight_ref[...], totals[32:], row_sum)
    new_pixel_ref[...] = new_pixel
    new_dual_ref[...] = new_dual
    rows = marks_ref.shape[0]
    marks = positions(marks_ref[...])
    q, h = kinds(rows)
    key = jnp.where((marks >= 0.0) & (q == 0.0), marks * 2.0 + h, -1.0)
    onehot = (iota((rows, 128), 1).astype(F32) == key).astype(BF16)[:, :32]
    out_ref[...] = dot(onehot, new_dual.astype(BF16))


def pull_kernel(x_ref, cov_ref, out_ref):
    out_ref[...] = jnp.broadcast_to(pull(x_ref, cov_ref), out_ref.shape)


def push_kernel(in_ref, price_ref, site_ref, sum_ref, cov_ref, out_ref, new_ref):
    totals = jnp.sum(in_ref[...].reshape(-1, 8, 128), axis=0)
    new = jnp.clip(site_ref[...] - (price_ref[...] - totals[0:1] / sum_ref[...]), 0.0, 1.0)
    new_ref[...] = new
    push(2.0 * new - site_ref[...], False, cov_ref, out_ref)


def spread_kernel(x_ref, marks_ref, out_ref):
    rows = x_ref.shape[0]
    marks = positions(marks_ref[...])
    q, h = kinds(rows)
    key = jnp.where((marks >= 0.0) & (q == 0.0), marks * 2.0 + h, -1.0)
    onehot = (iota((rows, 128), 1).astype(F32) == key).astype(BF16)[:, :32]
    spread = exact_pick(onehot, x_ref[...], ((0,), (0,)))
    for s in range(out_ref.shape[0]):
        out_ref[s] = spread


def dual_kernel(in_ref, row_ref, dual_ref, weight_ref, pixel_ref, new_dual_ref, new_pixel_ref):
    pushed = jnp.sum(in_ref[...], axis=0)
    new_pixel_ref[...], new_dual_ref[...] = step(
        pixel_ref[...], dual_ref[...], weight_ref[...], pushed, row_ref[...]
    )


def local(
    n_pix,
    n_site,
    margins,
    block_pos,
    pattern_ids,
    pattern_gain,
    site_price,
    weights,
    site_start,
    pixel_start,
    dual_start,
):
    slots = margins.shape[0]
    rows = 4 * slots
    chunks = 16
    to_pix = lambda x: lax.all_to_all(x.reshape(n_pix, -1, 128), "pix", 0, 0, tiled=True).reshape(-1, 128)
    to_site = lambda x: lax.all_to_all(x, "site", 0, 0, tiled=True)
    price, site0 = site_price.reshape(1, 128), site_start.reshape(1, 128)
    dual0, weight, pixel0 = (v.reshape(32, 128) for v in (dual_start, weights, pixel_start))

    copies = jnp.broadcast_to(dual0.astype(BF16)[None], (n_pix, 32, 128))
    gathered = to_pix(copies)
    hbm = pl.BlockSpec(memory_space=pl.ANY)
    cov, sums, marks = call(
        functools.partial(build_kernel, chunks),
        [((slots // 2, 256, 256), BF16), ((8, 128), F32), ((rows, 128), F32)],
        margins,
        block_pos,
        pattern_ids.reshape(1, 128),
        pattern_gain,
        scratch=[
            pltpu.VMEM(margins.shape, jnp.int32),
            pltpu.VMEM((256, 128), F32),
            pltpu.SemaphoreType.DMA((chunks,)),
        ],
        specs=[hbm, VMEM, VMEM, VMEM],
        flops=10 * margins.size,
        nbytes=6 * margins.size,
    )
    message = ((rows, 128), F32)
    (out,) = call(first_pull_kernel, [message], gathered, marks, cov, sums, scratch=[pltpu.VMEM((rows, 128), F32)])
    summed = to_pix(out)
    out, site1, column_sum = call(
        first_push_kernel, [message, ((1, 128), F32), ((1, 128), F32)], summed, price, site0, cov
    )
    (out,) = call(first_spread_kernel, [((n_site, 64, 128), F32)], to_pix(out), summed)
    out, dual1, pixel1, row_sum = call(
        first_dual_kernel, [message] + [((32, 128), F32)] * 3, to_site(out), summed, dual0, weight, pixel0
    )
    (out,) = call(pull_kernel, [message], to_pix(out), cov)
    out, site2 = call(push_kernel, [message, ((1, 128), F32)], to_pix(out), price, site1, column_sum, cov)
    (out,) = call(spread_kernel, [((n_site, 32, 128), F32)], to_pix(out), summed)
    dual2, pixel2 = call(dual_kernel, [((32, 128), F32)] * 2, to_site(out), row_sum, dual1, weight, pixel1)
    return site2.reshape(-1), pixel2.reshape(-1), dual2.reshape(-1)


def solution(mesh):
    placed = (
        P("pix", None, "site"),
        P("pix", "site"),
        P("site"),
        P(),
        P("site"),
        P("pix"),
        P("site"),
        P("pix"),
        P("pix"),
    )
    return jax.shard_map(
        functools.partial(local, mesh.shape["pix"], mesh.shape["site"]),
        mesh=mesh,
        in_specs=placed,
        out_specs=(P("site"), P("pix"), P("pix")),
        check_vma=False,
    )
```

time: 285 us -> 118 us (0.41); the launches traced: 279 us -> 118 us
  blocking collectives: 182 us -> 90.3 us
  waiting for transfers between devices: 50.3 us -> 0.57 us
  matrix products: 20.9 us -> 0 us
  Pallas kernels: 0 us -> 9.78 us
  other arithmetic: 8.33 us -> 0.73 us
  starting transfers between devices: 16.1 us -> 8.58 us
  local copies, waits for them, and re-layouts: 1.03 us -> 7.03 us
    psum x4 -> x0, blocking collectives: 182 us -> none  [the longest x2 136 us: column_totals(): return lax.psum(partial_value, 'pix')]
    all_to_all x0 -> x7, blocking collectives: none -> 90.3 us  [the longest x5 60.7 us: local(): lax.all_to_all(x.reshape(n_pix, -1, 128), 'pix', 0, 0, tiled=True)]
    all_to_all x2 -> x1, waiting for transfers between devices: 50.3 us -> 0.57 us  [local(): lax.all_to_all(x.reshape(n_pix, -1, 128), 'pix', 0, 0, tiled=True)]
    dot_general x12 -> x0, matrix products: 20.9 us -> none  [the longest x3 10.1 us: row_totals(): jnp.einsum('krj,tj->tkr', tiles_here, values, preferred_element_type=jnp....]
    pallas_call x0 -> x9, Pallas kernels: none -> 9.78 us  [call(): pl.pallas_call(body, out_shape=[jax.ShapeDtypeStruct(s, d) for s, d in ou...]
    all_to_all x2 -> x1, starting transfers between devices: 16.1 us -> 8.58 us  [local(): lax.all_to_all(x.reshape(n_pix, -1, 128), 'pix', 0, 0, tiled=True)]
    convert_element_type x5 -> x1, other arithmetic: 7.01 us -> 0.73 us  [local(): copies = jnp.broadcast_to(dual0.astype(BF16)[None], (n_pix, 32, 128))]
    unnamed x17 -> x21, local copies, waits for them, and re-layouts: 0.09 us -> 6.29 us
  transfers between devices with their start and end apart: 2 -> 1, of which waited for: 1 -> 1; matrix products, arithmetic and copies ran while one was open for 3% -> 1% of each run, Pallas kernels for 0% -> 4%
where the time goes in v1:
time: 118 us
  blocking collectives  90.3 us (77%)
  Pallas kernels  9.78 us (8%)
  starting transfers between devices  8.58 us (7%)
  local copies, waits for them, and re-layouts  7.03 us (6%)
    all_to_all x5, blocking collectives, local(): lax.all_to_all(x.reshape(n_pix, -1, 128), 'pix', 0, 0, tiled=True)  60.7 us
    all_to_all x2, blocking collectives, local(): to_site = lambda x: lax.all_to_all(x, 'site', 0, 0, tiled=True)  29.6 us
    pallas_call x9, Pallas kernels, call(): pl.pallas_call(body, out_shape=[jax.ShapeDtypeStruct(s, d) for s, d in ou...  9.78 us
    all_to_all x1, starting transfers between devices, local(): lax.all_to_all(x.reshape(n_pix, -1, 128), 'pix', 0, 0, tiled=True)  8.58 us
    unnamed x21, local copies, waits for them, and re-layouts  6.29 us
  transfers between devices with their start and end apart: 1, of which 1 were waited for; matrix products, arithmetic and copies ran while one was open for 1% of the time, Pallas kernels for 4%

profile of v1, /device:TPU:1, one launch (start us, length us, event | category | flops | bytes accessed | tf_op | source)
XLA Modules:
  0.0 117.7 jit_solution(10348303232362651582)
XLA Ops:
  0.6 0.0 copy-start.9
  0.6 0.0 copy-start.7
  0.7 0.7 bitcast_convert_fusion
  1.4 0.7 broadcast_in_dim.2
  2.1 8.6 %all-to-all-start = ((bf16[32,32,128]{2,1,0:T(8,128)(2,1)}), bf16[32,32,128]{2,1,0:T(8,128)(2,1)S(1)}, u32[]{:S(2)}, u32[]{:S(2)}) async-start(bf16[32,32,128]{2,1,0:T(8,128)(2,1)} %broadcast_in_dim.2), calls=%async_computation | async-start | bytes 524288 | tf_op jit(solution)/shard_map/all_to_all | solution.py:225
  10.7 0.7 copy.12.pos_ref
  11.5 0.0 copy-start.5
  11.5 0.7 copy-done.5
  12.2 0.0 copy-start.8
  12.2 0.7 copy-done.8
  12.8 0.0 copy-start.3
  12.8 0.0 copy-start.4
  12.8 0.0 copy-start.6
  12.8 4.2 %shard_map.112 = (bf16[32,256,256]{2,1,0:T(8,128)(2,1)S(1)}, f32[8,128]{1,0:T(8,128)S(1)}, f32[256,128]{1,0:T(8,128)S(1)}) custom-call(s32[64,256,128]{2,1,0:T(8,128)} %m_hbm.1, s32[64,1]{1,0:T(8,128)S(1)} %copy.12.pos_ref, s32[1,128]{1,0:T(1,128)S(1)} %bitcast.41, f32[16,256]{1,0:T(8,128)S(1)} %copy-done.5), custom_call_target="tpu_custom_call" | custom-call | flops 20971520 | bytes 12582912 | tf_op jit(solution)/shard_map/pallas_call | solution.py:33
  17.0 0.0 copy-start
  17.0 2.0 %copy-done = bf16[32,256,256]{2,1,0:T(8,128)(2,1)} copy-done((bf16[32,256,256]{2,1,0:T(8,128)(2,1)}, bf16[32,256,256]{2,1,0:T(8,128)(2,1)S(1)}, u32[]{:S(2)}) %copy-start) | copy-done | bytes 4194328
  19.0 0.6 all-to-all-done
  19.6 0.0 copy-start.1
  19.6 2.2 %copy-done.1 = bf16[32,256,256]{2,1,0:T(8,128)(2,1)S(1)} copy-done((bf16[32,256,256]{2,1,0:T(8,128)(2,1)S(1)}, bf16[32,256,256]{2,1,0:T(8,128)(2,1)}, u32[]{:S(2)}) %copy-start.1) | copy-done | bytes 4194328
  21.8 0.0 copy-start.2
  21.8 1.2 %shard_map.113 = f32[256,128]{1,0:T(8,128)S(1)} custom-call(bf16[1024,128]{1,0:T(8,128)(2,1)S(1)} %bitcast.25, f32[256,128]{1,0:T(8,128)S(1)} %get-tuple-element.17.map_ref, bf16[32,256,256]{2,1,0:T(8,128)(2,1)S(1)} %copy-done.1, f32[8,128]{1,0:T(8,128)S(1)} %get-tuple-element.19.sum_ref), custom_call_target="tpu_custom_call" | custom-call | tf_op jit(solution)/shard_map/pallas_call | solution.py:33
  23.0 14.3 %all_to_all.40 = f32[32,8,128]{2,1,0:T(8,128)S(1)} all-to-all(f32[32,8,128]{2,1,0:T(8,128)S(1)} %bitcast.27), channel_id=1, replica_groups=mesh['pix'=32,'site'=8] {'pix'}, dimensions={0} | all-to-all | bytes 262144 | tf_op jit(solution)/shard_map/all_to_all | solution.py:225
  37.3 0.0 copy-done.9
  37.3 0.0 copy-done.7
  37.3 1.2 %shard_map.114 = (f32[256,128]{1,0:T(8,128)S(1)}, f32[1,128]{1,0:T(1,128)S(1)}, f32[1,128]{1,0:T(1,128)S(1)}) custom-call(f32[256,128]{1,0:T(8,128)S(1)} %bitcast.21, f32[1,128]{1,0:T(1,128)S(1)} %bitcast.39, f32[1,128]{1,0:T(1,128)S(1)} %bitcast.42, bf16[32,256,256]{2,1,0:T(8,128)(2,1)S(1)} %copy-done.1), custom_call_target="tpu_custom_call" | custom-call | tf_op jit(solution)/shard_map/pallas_call | solution.py:33
  38.5 11.3 %all_to_all.41 = f32[32,8,128]{2,1,0:T(8,128)S(1)} all-to-all(f32[32,8,128]{2,1,0:T(8,128)S(1)} %bitcast.34), channel_id=1, replica_groups=mesh['pix'=32,'site'=8] {'pix'}, dimensions={0} | all-to-all | bytes 262144 | tf_op jit(solution)/shard_map/all_to_all | solution.py:225
  49.8 0.3 shard_map.115
  50.0 19.0 %all_to_all.42.in_ref = f32[8,64,128]{2,1,0:T(8,128)S(1)} all-to-all(f32[8,64,128]{2,1,0:T(8,128)S(1)} %shard_map.115), channel_id=1, replica_groups=mesh['pix'=32,'site'=8] {'site'}, dimensions={0} | all-to-all | bytes 524288 | tf_op jit(solution)/shard_map/all_to_all | solution.py:226
  69.0 0.0 copy-done.3
  69.0 0.0 copy-done.4
  69.0 0.0 copy-done.6
  69.0 0.2 shard_map.116
  69.2 12.6 %all_to_all.43 = f32[32,8,128]{2,1,0:T(8,128)S(1)} all-to-all(f32[32,8,128]{2,1,0:T(8,128)S(1)} %bitcast.33), channel_id=1, replica_groups=mesh['pix'=32,'site'=8] {'pix'}, dimensions={0} | all-to-all | bytes 262144 | tf_op jit(solution)/shard_map/all_to_all | solution.py:225
  81.8 0.0 copy-done.2
  81.8 0.7 shard_map.117
  82.4 11.2 %all_to_all.44 = f32[32,8,128]{2,1,0:T(8,128)S(1)} all-to-all(f32[32,8,128]{2,1,0:T(8,128)S(1)} %bitcast.30), channel_id=1, replica_groups=mesh['pix'=32,'site'=8] {'pix'}, dimensions={0} | all-to-all | bytes 262144 | tf_op jit(solution)/shard_map/all_to_all | solution.py:225
  93.7 1.2 %shard_map.118 = (f32[256,128]{1,0:T(8,128)S(1)}, f32[1,128]{1,0:T(1,128)}) custom-call(f32[256,128]{1,0:T(8,128)S(1)} %bitcast.26, f32[1,128]{1,0:T(1,128)S(1)} %bitcast.40, f32[1,128]{1,0:T(1,128)S(1)} %get-tuple-element.22.site_ref, f32[1,128]{1,0:T(1,128)S(1)} %get-tuple-element.23.sum_ref, bf16[32,256,256]{2,1,0:T(8,128)(2,1)S(1)} %copy-done.2), custom_call_target="tpu_custom_call" | custom-call | tf_op jit(solution)/shard_map/pallas_call | solution.py:33
  94.9 11.3 %all_to_all.45 = f32[32,8,128]{2,1,0:T(8,128)S(1)} all-to-all(f32[32,8,128]{2,1,0:T(8,128)S(1)} %bitcast.32), channel_id=1, replica_groups=mesh['pix'=32,'site'=8] {'pix'}, dimensions={0} | all-to-all | bytes 262144 | tf_op jit(solution)/shard_map/all_to_all | solution.py:225
  106.1 0.3 shard_map.119
  106.4 10.7 %all_to_all.46.in_ref = f32[8,32,128]{2,1,0:T(8,128)S(1)} all-to-all(f32[8,32,128]{2,1,0:T(8,128)S(1)} %shard_map.119), channel_id=1, replica_groups=mesh['pix'=32,'site'=8] {'site'}, dimensions={0} | all-to-all | bytes 262144 | tf_op jit(solution)/shard_map/all_to_all | solution.py:226
  117.1 0.6 shard_map.120
Async XLA Ops:
  0.6 36.7 %copy-start.9 = (f32[128]{0:T(128)S(1)}, f32[128]{0:T(128)}, u32[]{:S(2)}) copy-start(f32[128]{0:T(128)} %param.15) | copy-start | bytes 1540
  0.6 36.7 %copy-start.7 = (f32[128]{0:T(128)S(1)}, f32[128]{0:T(128)}, u32[]{:S(2)}) copy-start(f32[128]{0:T(128)} %param.13) | copy-start | bytes 1540
  2.1 17.5 %all-to-all-start = ((bf16[32,32,128]{2,1,0:T(8,128)(2,1)}), bf16[32,32,128]{2,1,0:T(8,128)(2,1)S(1)}, u32[]{:S(2)}, u32[]{:S(2)}) async-start(bf16[32,32,128]{2,1,0:T(8,128)(2,1)} %broadcast_in_dim.2), calls=%async_computation | async-start | bytes 524288 | tf_op jit(solution)/shard_map/all_to_all | solution.py:225
  11.5 0.7 copy-start.5
  12.2 0.7 copy-start.8
  12.8 56.2 %copy-start.3 = (f32[4096]{0:T(1024)S(1)}, f32[4096]{0:T(1024)}, u32[]{:S(2)}) copy-start(f32[4096]{0:T(1024)} %param.14) | copy-start | bytes 49156
  12.8 56.2 %copy-start.4 = (f32[4096]{0:T(1024)S(1)}, f32[4096]{0:T(1024)}, u32[]{:S(2)}) copy-start(f32[4096]{0:T(1024)} %param.17) | copy-start | bytes 49156
  12.8 56.2 %copy-start.6 = (f32[4096]{0:T(1024)S(1)}, f32[4096]{0:T(1024)}, u32[]{:S(2)}) copy-start(f32[4096]{0:T(1024)} %param.16) | copy-start | bytes 49156
  17.0 2.0 %copy-start = (bf16[32,256,256]{2,1,0:T(8,128)(2,1)}, bf16[32,256,256]{2,1,0:T(8,128)(2,1)S(1)}, u32[]{:S(2)}) copy-start(bf16[32,256,256]{2,1,0:T(8,128)(2,1)S(1)} %get-tuple-element.18.cov_ref) | copy-start | bytes 12582916
  19.6 2.2 %copy-start.1 = (bf16[32,256,256]{2,1,0:T(8,128)(2,1)S(1)}, bf16[32,256,256]{2,1,0:T(8,128)(2,1)}, u32[]{:S(2)}) copy-start(bf16[32,256,256]{2,1,0:T(8,128)(2,1)} %copy-done) | copy-start | bytes 12582916
  21.8 60.0 %copy-start.2 = (bf16[32,256,256]{2,1,0:T(8,128)(2,1)S(1)}, bf16[32,256,256]{2,1,0:T(8,128)(2,1)}, u32[]{:S(2)}) copy-start(bf16[32,256,256]{2,1,0:T(8,128)(2,1)} %copy-done) | copy-start | bytes 12582916

commit v2 on v1

--- a/solution.py
+++ b/solution.py
@@ -11,6 +11,7 @@
 BF16 = jnp.bfloat16
 HALF_SCALE = 2.0 ** (-10)
 VMEM = pl.BlockSpec(memory_space=pltpu.VMEM)
+HBM = pl.BlockSpec(memory_space=pltpu.HBM)
 
 
 def iota(shape, dim):
@@ -29,51 +30,112 @@
     return dot(onehot, high, dims) + (dot(onehot, middle, dims) + dot(onehot, low, dims))
 
 
-def call(body, outs, *args, scratch=(), specs=None, flops=0, nbytes=0):
+def call(body, outs, *args, scratch=(), specs=None, flops=0, nbytes=0, mib=8):
     return pl.pallas_call(
         body,
-        out_shape=[jax.ShapeDtypeStruct(s, d) for s, d in outs],
+        out_shape=[o if hasattr(o, "memory_space") else jax.ShapeDtypeStruct(*o) for o in outs],
         in_specs=specs or [VMEM] * len(args),
-        out_specs=[VMEM] * len(outs),
+        out_specs=[HBM if hasattr(o, "memory_space") else VMEM for o in outs],
         scratch_shapes=list(scratch),
         cost_estimate=pl.CostEstimate(flops=flops, transcendentals=0, bytes_accessed=nbytes),
-        compiler_params=pltpu.CompilerParams(vmem_limit_bytes=48 * 1024 * 1024),
+        compiler_params=pltpu.CompilerParams(vmem_limit_bytes=mib * 1024 * 1024),
     )(*args)
 
 
-def build_kernel(chunks, m_hbm, pos_ref, ids_ref, gain_ref, cov_ref, sum_ref, map_ref, buf, half_gain, sems):
+def in_hbm(value):
+    return pltpu.with_memory_space_constraint(value, pltpu.HBM)
+
+
+def prepare_kernel(dual_hbm, out_ref, dual_ref, sem):
+    copy = pltpu.make_async_copy(dual_hbm, dual_ref, sem)
+    copy.start()
+    copy.wait()
+    dual = dual_ref[...].astype(BF16)
+    for t in range(out_ref.shape[0]):
+        out_ref[t] = dual
+
+
+def build_kernel(
+    chunks,
+    m_hbm,
+    pos_hbm,
+    ids_hbm,
+    gain_hbm,
+    near_ref,
+    far_hbm,
+    sum_ref,
+    map_ref,
+    pick_ref,
+    buf,
+    far_ref,
+    half_gain,
+    pos_ref,
+    ids_ref,
+    gain_ref,
+    sems,
+    small_sems,
+    far_sems,
+):
+    small = [(pos_hbm, pos_ref), (ids_hbm, ids_ref), (gain_hbm, gain_ref)]
+    small = [pltpu.make_async_copy(src, dst, small_sems.at[n]) for n, (src, dst) in enumerate(small)]
+    for copy in small:
+        copy.start()
     slots = m_hbm.shape[0]
     per = slots // chunks
-    copies = []
-    for c in range(chunks):
+    copies = {}
+    for c in reversed(range(chunks)):
         part = pl.ds(c * per, per)
         copy = pltpu.make_async_copy(m_hbm.at[part], buf.at[part], sems.at[c])
         copy.start()
-        copies.append(copy)
+        copies[c] = copy
+    for copy in small:
+        copy.wait()
     patterns = gain_ref.shape[0]
     onehot = (ids_ref[...] == iota((patterns, 128), 0)).astype(BF16)
     half_gain[...] = 0.5 * gain_pick(gain_ref[...], onehot)
     rows = 4 * slots
     expand = (iota((rows, slots), 1) == (iota((rows, slots), 0) >> 2)).astype(BF16)
-    wide = jnp.broadcast_to(pos_ref[...].astype(F32), (slots, 128)).astype(BF16)
-    map_ref[...] = dot(expand, wide)
+    wide = jnp.broadcast_to(pos_ref[...].astype(F32), (128, slots)).astype(BF16)
+    marks = dot(expand, wide, ((1,), (1,)))
+    map_ref[...] = marks
+    q, h = kinds(rows)
+    tile = (iota((rows, 128), 0) >> 3).astype(F32)
+    key = jnp.where((marks >= 0.0) & (q == 0.0), tile * 32.0 + marks * 2.0 + h, -1.0)
+    for c in range(pick_ref.shape[1] // 128):
+        lane = (iota((rows, 128), 1) + c * 128).astype(F32)
+        pick_ref[:, c * 128 : (c + 1) * 128] = (lane == key).astype(BF16)
     sum_ref[...] = jnp.zeros_like(sum_ref)
-    for c in range(chunks):
-        copies[c].wait()
-
+    near = near_ref.shape[0]
+    sent = []
+
+    def pairs(first, last, out_ref, offset):
         def pair(t, carry):
             marks = map_ref[pl.ds(pl.multiple_of(t * 8, 8), 8), :]
             total = jnp.zeros((8, 128), F32)
             for i in range(2):
                 level = buf[2 * t + i].astype(F32) * HALF_SCALE + half_gain[...]
                 tile = (0.5 * jnp.tanh(level) + 0.5).astype(BF16)
-                cov_ref[t, :, i * 128 : (i + 1) * 128] = tile
+                out_ref[t - offset, :, i * 128 : (i + 1) * 128] = tile
                 part = jnp.sum(tile.astype(F32).reshape(-1, 8, 128), axis=0)
                 total = total + jnp.where(marks[4 * i : 4 * i + 1] >= 0.0, part, 0.0)
             sum_ref[...] += total
             return carry
 
-        lax.fori_loop(c * per // 2, (c + 1) * per // 2, pair, 0)
+        lax.fori_loop(first, last, pair, 0)
+
+    for c in reversed(range(chunks)):
+        copies[c].wait()
+        first, last = c * per // 2, (c + 1) * per // 2
+        if first >= near:
+            pairs(first, last, far_ref, near)
+            part = pl.ds(first - near, last - first)
+            copy = pltpu.make_async_copy(far_ref.at[part], far_hbm.at[part], far_sems.at[c])
+            copy.start()
+            sent.append(copy)
+        else:
+            pairs(first, last, near_ref, 0)
+    for copy in sent:
+        copy.wait()
 
 
 def gain_pick(gain, onehot):
@@ -85,26 +147,30 @@
     return dot(high, onehot, dims) + (dot(middle, onehot, dims) + dot(low, onehot, dims))
 
 
-def pull(x_ref, cov_ref):
+def tiles(*refs):
+    return [ref.at[t] for ref in refs for t in range(ref.shape[0])]
+
+
+def pull(x_ref, cov):
     first = (iota((8, 128), 0) & 2) == 0
     total = jnp.zeros((8, 256), F32)
-    for t in range(cov_ref.shape[0]):
+    for t, tile in enumerate(cov):
         x = x_ref[t * 8 : (t + 1) * 8, :]
         left = jnp.concatenate([jnp.where(first, x, 0.0), jnp.where(first, 0.0, x)], axis=1)
-        total = total + dot(left.astype(BF16), cov_ref[t])
+        total = total + dot(left.astype(BF16), tile[...])
     own = jnp.where(iota((8, 128), 0) < 4, total[:, :128], total[:, 128:])
     return jnp.sum(own, axis=0, keepdims=True)
 
 
-def push(row, plain, cov_ref, out_ref):
+def push(row, plain, cov, out_ref):
     spot = iota((8, 128), 0)
     value = jnp.broadcast_to(row, (8, 128))
     if plain:
         value = jnp.where((spot & 1) == 1, value, 1.0)
     left = jnp.concatenate([jnp.where(spot < 4, value, 0.0), jnp.where(spot < 4, 0.0, value)], axis=1).astype(BF16)
     first = (spot & 2) == 0
-    for t in range(cov_ref.shape[0]):
-        product = dot(left, cov_ref[t], ((1,), (1,)))
+    for t, tile in enumerate(cov):
+        product = dot(left, tile[...], ((1,), (1,)))
         out_ref[t * 8 : (t + 1) * 8, :] = jnp.where(first, product[:, :128], product[:, 128:])
 
 
@@ -119,31 +185,28 @@
     return (spot & 1).astype(F32), ((spot >> 1) & 1).astype(F32)
 
 
-def first_pull_kernel(ag_ref, map_ref, cov_ref, sum_ref, out_ref, x_ref):
-    rows = map_ref.shape[0]
-    marks = map_ref[...]
-    q, h = kinds(rows)
-    tile = (iota((rows, 128), 0) >> 3).astype(F32)
-    key = jnp.where((marks >= 0.0) & (q == 0.0), tile * 32.0 + marks * 2.0 + h, -1.0)
-    picked = jnp.zeros((rows, 128), F32)
-    for c in range(ag_ref.shape[0] // 128):
-        lane = (iota((rows, 128), 1) + c * 128).astype(F32)
-        picked = picked + dot((lane == key).astype(BF16), ag_ref[c * 128 : (c + 1) * 128, :])
-    x_ref[...] = picked
-    pulled = pull(x_ref, cov_ref)
+def first_pull_kernel(ag_ref, pick_ref, map_ref, near_ref, far_hbm, sum_ref, out_ref, far_ref, x_ref, sem):
+    copy = pltpu.make_async_copy(far_hbm, far_ref, sem)
+    copy.start()
+    x_ref[...] = dot(pick_ref[...], ag_ref[...])
+    near = near_ref.shape[0]
+    pulled = pull(x_ref, tiles(near_ref))
+    copy.wait()
+    pulled = pulled + pull(x_ref.at[near * 8 :], tiles(far_ref))
     sums = jnp.sum(sum_ref[...], axis=0, keepdims=True)
-    tiles = marks.reshape(-1, 8, 128)
-    spot = iota(tiles.shape, 1)
-    out_ref[...] = jnp.where(spot == 0, sums[None], jnp.where(spot == 1, pulled[None], tiles)).reshape(rows, 128)
-
-
-def first_push_kernel(in_ref, price_ref, site_ref, cov_ref, out_ref, new_ref, sum_ref):
+    marks = map_ref[...].reshape(-1, 8, 128)
+    spot = iota(marks.shape, 1)
+    out = jnp.where(spot == 0, sums[None], jnp.where(spot == 1, pulled[None], marks))
+    out_ref[...] = out.reshape(out_ref.shape)
+
+
+def first_push_kernel(in_ref, price_ref, site_ref, near_ref, far_ref, out_ref, new_ref, sum_ref):
     totals = jnp.sum(in_ref[...].reshape(-1, 8, 128), axis=0)
     column_sum = totals[0:1]
     new = jnp.clip(site_ref[...] - (price_ref[...] - totals[1:2] / column_sum), 0.0, 1.0)
     new_ref[...] = new
     sum_ref[...] = column_sum
-    push(2.0 * new - site_ref[...], True, cov_ref, out_ref)
+    push(2.0 * new - site_ref[...], True, tiles(near_ref, far_ref), out_ref)
 
 
 def first_spread_kernel(x_ref, marks_ref, out_ref):
@@ -177,15 +240,15 @@
     out_ref[...] = dot(onehot, new_dual.astype(BF16))
 
 
-def pull_kernel(x_ref, cov_ref, out_ref):
-    out_ref[...] = jnp.broadcast_to(pull(x_ref, cov_ref), out_ref.shape)
-
-
-def push_kernel(in_ref, price_ref, site_ref, sum_ref, cov_ref, out_ref, new_ref):
+def pull_kernel(x_ref, near_ref, far_ref, out_ref):
+    out_ref[...] = jnp.broadcast_to(pull(x_ref, tiles(near_ref, far_ref)), out_ref.shape)
+
+
+def push_kernel(in_ref, price_ref, site_ref, sum_ref, near_ref, far_ref, out_ref, new_ref):
     totals = jnp.sum(in_ref[...].reshape(-1, 8, 128), axis=0)
     new = jnp.clip(site_ref[...] - (price_ref[...] - totals[0:1] / sum_ref[...]), 0.0, 1.0)
     new_ref[...] = new
-    push(2.0 * new - site_ref[...], False, cov_ref, out_ref)
+    push(2.0 * new - site_ref[...], False, tiles(near_ref, far_ref), out_ref)
 
 
 def spread_kernel(x_ref, marks_ref, out_ref):
@@ -227,37 +290,69 @@
     price, site0 = site_price.reshape(1, 128), site_start.reshape(1, 128)
     dual0, weight, pixel0 = (v.reshape(32, 128) for v in (dual_start, weights, pixel_start))
 
-    copies = jnp.broadcast_to(dual0.astype(BF16)[None], (n_pix, 32, 128))
+    pairs, near = slots // 2, slots * 9 // 32 // 2 * 2
+    far = pairs - near
+    (copies,) = call(
+        prepare_kernel,
+        [((n_pix, 32, 128), BF16)],
+        in_hbm(dual0),
+        scratch=[pltpu.VMEM((32, 128), F32), pltpu.SemaphoreType.DMA],
+        specs=[HBM],
+    )
     gathered = to_pix(copies)
-    hbm = pl.BlockSpec(memory_space=pl.ANY)
-    cov, sums, marks = call(
+    near_tiles, far_tiles, sums, marks, pick = call(
         functools.partial(build_kernel, chunks),
-        [((slots // 2, 256, 256), BF16), ((8, 128), F32), ((rows, 128), F32)],
-        margins,
-        block_pos,
-        pattern_ids.reshape(1, 128),
-        pattern_gain,
+        [
+            ((near, 256, 256), BF16),
+            pltpu.HBM((far, 256, 256), BF16),
+            ((8, 128), F32),
+            ((rows, 128), F32),
+            ((rows, 32 * n_pix), BF16),
+        ],
+        *(
+            in_hbm(v)
+            for v in (margins, block_pos.reshape(1, slots), pattern_ids.reshape(1, 128), pattern_gain)
+        ),
         scratch=[
             pltpu.VMEM(margins.shape, jnp.int32),
+            pltpu.VMEM((far, 256, 256), BF16),
             pltpu.VMEM((256, 128), F32),
+            pltpu.VMEM((1, slots), jnp.int32),
+            pltpu.VMEM((1, 128), jnp.int32),
+            pltpu.VMEM(pattern_gain.shape, F32),
+            pltpu.SemaphoreType.DMA((chunks,)),
+            pltpu.SemaphoreType.DMA((3,)),
             pltpu.SemaphoreType.DMA((chunks,)),
         ],
-        specs=[hbm, VMEM, VMEM, VMEM],
+        specs=[HBM] * 4,
         flops=10 * margins.size,
         nbytes=6 * margins.size,
+        mib=24,
     )
     message = ((rows, 128), F32)
-    (out,) = call(first_pull_kernel, [message], gathered, marks, cov, sums, scratch=[pltpu.VMEM((rows, 128), F32)])
+    out, far_tiles = call(
+        first_pull_kernel,
+        [message, ((far, 256, 256), BF16)],
+        gathered,
+        pick,
+        marks,
+        near_tiles,
+        in_hbm(far_tiles),
+        sums,
+        scratch=[pltpu.VMEM((rows, 128), F32), pltpu.SemaphoreType.DMA],
+        specs=[VMEM] * 4 + [HBM, VMEM],
+    )
+    cov = (near_tiles, far_tiles)
     summed = to_pix(out)
     out, site1, column_sum = call(
-        first_push_kernel, [message, ((1, 128), F32), ((1, 128), F32)], summed, price, site0, cov
+        first_push_kernel, [message, ((1, 128), F32), ((1, 128), F32)], summed, price, site0, *cov
     )
     (out,) = call(first_spread_kernel, [((n_site, 64, 128), F32)], to_pix(out), summed)
     out, dual1, pixel1, row_sum = call(
         first_dual_kernel, [message] + [((32, 128), F32)] * 3, to_site(out), summed, dual0, weight, pixel0
     )
-    (out,) = call(pull_kernel, [message], to_pix(out), cov)
-    out, site2 = call(push_kernel, [message, ((1, 128), F32)], to_pix(out), price, site1, column_sum, cov)
+    (out,) = call(pull_kernel, [message], to_pix(out), *cov)
+    out, site2 = call(push_kernel, [message, ((1, 128), F32)], to_pix(out), price, site1, column_sum, *cov)
     (out,) = call(spread_kernel, [((n_site, 32, 128), F32)], to_pix(out), summed)
     dual2, pixel2 = call(dual_kernel, [((32, 128), F32)] * 2, to_site(out), row_sum, dual1, weight, pixel1)
     return site2.reshape(-1), pixel2.reshape(-1), dual2.reshape(-1)

time: 118 us -> 115 us (0.975)
  local copies, waits for them, and re-layouts: 7.03 us -> 0.02 us
  Pallas kernels: 9.78 us -> 14.8 us
  blocking collectives: 90.3 us -> 88.6 us
  waiting for transfers between devices: 0.57 us -> 2.12 us
    unnamed x21 -> x10, local copies, waits for them, and re-layouts: 6.29 us -> 0.02 us
    pallas_call x9 -> x10, Pallas kernels: 9.78 us -> 14.8 us  [call(): pl.pallas_call(body, out_shape=[o if hasattr(o, 'memory_space') else jax....]
    all_to_all x5, blocking collectives: 60.7 us -> 59 us  [local(): lax.all_to_all(x.reshape(n_pix, -1, 128), 'pix', 0, 0, tiled=True)]
    all_to_all x1, waiting for transfers between devices: 0.57 us -> 2.12 us  [local(): lax.all_to_all(x.reshape(n_pix, -1, 128), 'pix', 0, 0, tiled=True)]
  transfers between devices with their start and end apart: 1 -> 1, of which waited for: 1 -> 1; matrix products, arithmetic and copies ran while one was open for 1% -> 0% of each run, Pallas kernels for 4% -> 6%
where the time goes in v2:
time: 115 us
  blocking collectives  88.6 us (77%)
  Pallas kernels  14.8 us (13%)
  starting transfers between devices  8.59 us (7%)
  waiting for transfers between devices  2.12 us (2%)
    all_to_all x5, blocking collectives, local(): lax.all_to_all(x.reshape(n_pix, -1, 128), 'pix', 0, 0, tiled=True)  59 us
    all_to_all x2, blocking collectives, local(): to_site = lambda x: lax.all_to_all(x, 'site', 0, 0, tiled=True)  29.6 us
    pallas_call x10, Pallas kernels, call(): pl.pallas_call(body, out_shape=[o if hasattr(o, 'memory_space') else jax....  14.8 us
    all_to_all x1, starting transfers between devices, local(): lax.all_to_all(x.reshape(n_pix, -1, 128), 'pix', 0, 0, tiled=True)  8.59 us
  transfers between devices with their start and end apart: 1, of which 1 were waited for; matrix products, arithmetic and copies ran while one was open for 0% of the time, Pallas kernels for 6%

profile of v2, /device:TPU:1, one launch (start us, length us, event | category | flops | bytes accessed | tf_op | source)
XLA Modules:
  0.0 114.8 jit_solution(12218775083748872915)
XLA Ops:
  0.6 1.5 %shard_map.112 = bf16[32,32,128]{2,1,0:T(8,128)(2,1)} custom-call(f32[32,128]{1,0:T(8,128)} %bitcast.35), custom_call_target="tpu_custom_call" | custom-call | tf_op jit(solution)/shard_map/pallas_call | solution.py:34
  2.1 8.6 %all-to-all-start = ((bf16[32,32,128]{2,1,0:T(8,128)(2,1)}), bf16[32,32,128]{2,1,0:T(8,128)(2,1)S(1)}, u32[]{:S(2)}, u32[]{:S(2)}) async-start(bf16[32,32,128]{2,1,0:T(8,128)(2,1)} %shard_map.112), calls=%async_computation | async-start | bytes 524288 | tf_op jit(solution)/shard_map/all_to_all | solution.py:288
  10.7 6.7 %shard_map.113 = (bf16[18,256,256]{2,1,0:T(8,128)(2,1)S(1)}, bf16[14,256,256]{2,1,0:T(8,128)(2,1)}, f32[8,128]{1,0:T(8,128)S(1)}, f32[256,128]{1,0:T(8,128)S(1)}, bf16[256,1024]{1,0:T(8,128)(2,1)S(1)}) custom-call(s32[64,256,128]{2,1,0:T(8,128)} %m_hbm.1, s32[1,64]{1,0:T(1,128)} %bitcast.43, s32[1,128]{1,0:T(1,128)} %bitcast.44, f32[16,256]{1,0:T(8,128)} %gain_hbm.1), custom_call_target="tpu_custom_call" | custom-call | flops 20971520 | bytes 12582912 | tf_op jit(solution)/shard_map/pallas_call | solution.py:34
  17.5 2.1 %all-to-all-done = bf16[32,32,128]{2,1,0:T(8,128)(2,1)S(1)} async-done(((bf16[32,32,128]{2,1,0:T(8,128)(2,1)}), bf16[32,32,128]{2,1,0:T(8,128)(2,1)S(1)}, u32[]{:S(2)}, u32[]{:S(2)}) %all-to-all-start) | async-done | bytes 262176 | tf_op jit(solution)/shard_map/all_to_all | solution.py:288
  19.6 0.0 copy-start.3
  19.6 0.0 copy-start.4
  19.6 2.1 %shard_map.114 = (f32[256,128]{1,0:T(8,128)S(1)}, bf16[14,256,256]{2,1,0:T(8,128)(2,1)S(1)}) custom-call(bf16[1024,128]{1,0:T(8,128)(2,1)S(1)} %bitcast.25, bf16[256,1024]{1,0:T(8,128)(2,1)S(1)} %get-tuple-element.21.pick_ref, f32[256,128]{1,0:T(8,128)S(1)} %get-tuple-element.22.map_ref, bf16[18,256,256]{2,1,0:T(8,128)(2,1)S(1)} %get-tuple-element.23.near_ref, ...), custom_call_target="tpu_custom_call" | custom-call | tf_op jit(solution)/shard_map/pallas_call | solution.py:34
  21.7 12.7 %all_to_all.40 = f32[32,8,128]{2,1,0:T(8,128)S(1)} all-to-all(f32[32,8,128]{2,1,0:T(8,128)S(1)} %bitcast.31), channel_id=1, replica_groups=mesh['pix'=32,'site'=8] {'pix'}, dimensions={0} | all-to-all | bytes 262144 | tf_op jit(solution)/shard_map/all_to_all | solution.py:288
  34.4 0.0 copy-done.3
  34.4 0.0 copy-done.4
  34.4 0.0 copy-start
  34.4 0.0 copy-start.1
  34.4 0.0 copy-start.2
  34.4 1.2 %shard_map.115 = (f32[256,128]{1,0:T(8,128)S(1)}, f32[1,128]{1,0:T(1,128)S(1)}, f32[1,128]{1,0:T(1,128)S(1)}) custom-call(f32[256,128]{1,0:T(8,128)S(1)} %bitcast.21, f32[1,128]{1,0:T(1,128)S(1)} %bitcast.40, f32[1,128]{1,0:T(1,128)S(1)} %bitcast.42, bf16[18,256,256]{2,1,0:T(8,128)(2,1)S(1)} %get-tuple-element.23.near_ref, ...), custom_call_target="tpu_custom_call" | custom-call | tf_op jit(solution)/shard_map/pallas_call | solution.py:34
  35.6 11.3 %all_to_all.41 = f32[32,8,128]{2,1,0:T(8,128)S(1)} all-to-all(f32[32,8,128]{2,1,0:T(8,128)S(1)} %bitcast.34), channel_id=1, replica_groups=mesh['pix'=32,'site'=8] {'pix'}, dimensions={0} | all-to-all | bytes 262144 | tf_op jit(solution)/shard_map/all_to_all | solution.py:288
  46.9 0.3 shard_map.116
  47.2 19.0 %all_to_all.42.in_ref = f32[8,64,128]{2,1,0:T(8,128)S(1)} all-to-all(f32[8,64,128]{2,1,0:T(8,128)S(1)} %shard_map.116), channel_id=1, replica_groups=mesh['pix'=32,'site'=8] {'site'}, dimensions={0} | all-to-all | bytes 524288 | tf_op jit(solution)/shard_map/all_to_all | solution.py:289
  66.1 0.0 copy-done
  66.1 0.0 copy-done.1
  66.1 0.0 copy-done.2
  66.1 0.2 shard_map.117
  66.3 12.6 %all_to_all.43 = f32[32,8,128]{2,1,0:T(8,128)S(1)} all-to-all(f32[32,8,128]{2,1,0:T(8,128)S(1)} %bitcast.33), channel_id=1, replica_groups=mesh['pix'=32,'site'=8] {'pix'}, dimensions={0} | all-to-all | bytes 262144 | tf_op jit(solution)/shard_map/all_to_all | solution.py:288
  78.9 0.7 shard_map.118
  79.6 11.2 %all_to_all.44 = f32[32,8,128]{2,1,0:T(8,128)S(1)} all-to-all(f32[32,8,128]{2,1,0:T(8,128)S(1)} %bitcast.29), channel_id=1, replica_groups=mesh['pix'=32,'site'=8] {'pix'}, dimensions={0} | all-to-all | bytes 262144 | tf_op jit(solution)/shard_map/all_to_all | solution.py:288
  90.8 1.2 %shard_map.119 = (f32[256,128]{1,0:T(8,128)S(1)}, f32[1,128]{1,0:T(1,128)}) custom-call(f32[256,128]{1,0:T(8,128)S(1)} %bitcast.26, f32[1,128]{1,0:T(1,128)S(1)} %bitcast.41, f32[1,128]{1,0:T(1,128)S(1)} %get-tuple-element.30.site_ref, f32[1,128]{1,0:T(1,128)S(1)} %get-tuple-element.31.sum_ref, bf16[18,256,256]{2,1,0:T(8,128)(2,1)S(1)} %get-tuple-element.23.near_ref, ...), custom_call_target="tpu_custom_call" | custom-call | tf_op jit(solution)/shard_map/pallas_call | solution.py:34
  92.0 11.3 %all_to_all.45 = f32[32,8,128]{2,1,0:T(8,128)S(1)} all-to-all(f32[32,8,128]{2,1,0:T(8,128)S(1)} %bitcast.32), channel_id=1, replica_groups=mesh['pix'=32,'site'=8] {'pix'}, dimensions={0} | all-to-all | bytes 262144 | tf_op jit(solution)/shard_map/all_to_all | solution.py:288
  103.3 0.3 shard_map.120
  103.5 10.7 %all_to_all.46.in_ref = f32[8,32,128]{2,1,0:T(8,128)S(1)} all-to-all(f32[8,32,128]{2,1,0:T(8,128)S(1)} %shard_map.120), channel_id=1, replica_groups=mesh['pix'=32,'site'=8] {'site'}, dimensions={0} | all-to-all | bytes 262144 | tf_op jit(solution)/shard_map/all_to_all | solution.py:289
  114.2 0.6 shard_map.121
Async XLA Ops:
  2.1 17.5 %all-to-all-start = ((bf16[32,32,128]{2,1,0:T(8,128)(2,1)}), bf16[32,32,128]{2,1,0:T(8,128)(2,1)S(1)}, u32[]{:S(2)}, u32[]{:S(2)}) async-start(bf16[32,32,128]{2,1,0:T(8,128)(2,1)} %shard_map.112), calls=%async_computation | async-start | bytes 524288 | tf_op jit(solution)/shard_map/all_to_all | solution.py:288
  19.6 14.8 %copy-start.3 = (f32[128]{0:T(128)S(1)}, f32[128]{0:T(128)}, u32[]{:S(2)}) copy-start(f32[128]{0:T(128)} %param.13) | copy-start | bytes 1540
  19.6 14.8 %copy-start.4 = (f32[128]{0:T(128)S(1)}, f32[128]{0:T(128)}, u32[]{:S(2)}) copy-start(f32[128]{0:T(128)} %param.15) | copy-start | bytes 1540
  34.4 31.7 %copy-start = (f32[4096]{0:T(1024)S(1)}, f32[4096]{0:T(1024)}, u32[]{:S(2)}) copy-start(f32[4096]{0:T(1024)} %param.17) | copy-start | bytes 49156
  34.4 31.7 %copy-start.1 = (f32[4096]{0:T(1024)S(1)}, f32[4096]{0:T(1024)}, u32[]{:S(2)}) copy-start(f32[4096]{0:T(1024)} %param.14) | copy-start | bytes 49156
  34.4 31.7 %copy-start.2 = (f32[4096]{0:T(1024)S(1)}, f32[4096]{0:T(1024)}, u32[]{:S(2)}) copy-start(f32[4096]{0:T(1024)} %param.16) | copy-start | bytes 49156

commit v3 on v2

v3 whole, which is shorter than its diff:
```python
import functools

import jax
import jax.numpy as jnp
from jax import lax
from jax.experimental import pallas as pl
from jax.experimental.pallas import tpu as pltpu
from jax.sharding import PartitionSpec as P

F32 = jnp.float32
BF16 = jnp.bfloat16
HALF_SCALE = 2.0 ** (-10)
VMEM = pl.BlockSpec(memory_space=pltpu.VMEM)
HBM = pl.BlockSpec(memory_space=pltpu.HBM)


def iota(shape, dim):
    return lax.broadcasted_iota(jnp.int32, shape, dim)


def dot(a, b, dims=((1,), (0,))):
    return lax.dot_general(a, b, (dims, ((), ())), preferred_element_type=F32)


def exact_pick(onehot, values, dims):
    high = values.astype(BF16)
    rest = values - high.astype(F32)
    middle = rest.astype(BF16)
    low = (rest - middle.astype(F32)).astype(BF16)
    return dot(onehot, high, dims) + (dot(onehot, middle, dims) + dot(onehot, low, dims))


def call(body, outs, *args, scratch=(), specs=None, flops=0, nbytes=0, mib=8):
    return pl.pallas_call(
        body,
        out_shape=[jax.ShapeDtypeStruct(*o) for o in outs],
        in_specs=specs or [VMEM] * len(args),
        out_specs=[VMEM] * len(outs),
        scratch_shapes=list(scratch),
        cost_estimate=pl.CostEstimate(flops=flops, transcendentals=0, bytes_accessed=nbytes),
        compiler_params=pltpu.CompilerParams(vmem_limit_bytes=mib * 1024 * 1024),
    )(*args)


def in_hbm(value):
    return pltpu.with_memory_space_constraint(value, pltpu.HBM)


def prepare_kernel(dual_hbm, out_ref, dual_ref, sem):
    copy = pltpu.make_async_copy(dual_hbm, dual_ref, sem)
    copy.start()
    copy.wait()
    dual = dual_ref[...].astype(BF16)
    for t in range(out_ref.shape[0]):
        out_ref[t] = dual


AHEAD = 6


def fetch(m_hbm, buf, sems, first, last):
    copies = []
    for c, t in enumerate(range(first, last, 2)):
        part = (m_hbm.at[pl.ds(2 * t, 4)], buf.at[pl.ds(2 * (t - first), 4)])
        copies.append(pltpu.make_async_copy(*part, sems.at[c]))
    for copy in copies[:AHEAD]:
        copy.start()
    return copies


def arrive(copies, c):
    copies[c].wait()
    for copy in copies[c + AHEAD : c + AHEAD + 1]:
        copy.start()


def build(buf, out_ref, half_gain, t):
    def pair(n, carry):
        gain = half_gain[...]
        level = jnp.concatenate([buf[2 * n + i].astype(F32) * HALF_SCALE + gain for i in range(2)], axis=1)
        out_ref[n] = (0.5 * jnp.tanh(level) + 0.5).astype(BF16)
        return carry

    pair(t, 0)
    pair(t + 1, 0)


def build_kernel(
    m_hbm,
    pos_hbm,
    ids_hbm,
    gain_hbm,
    near_ref,
    map_ref,
    note_ref,
    half_gain,
    buf,
    pos_ref,
    ids_ref,
    gain_ref,
    sems,
    small_sems,
):
    small = [(pos_hbm, pos_ref), (ids_hbm, ids_ref), (gain_hbm, gain_ref)]
    small = [pltpu.make_async_copy(src, dst, small_sems.at[n]) for n, (src, dst) in enumerate(small)]
    for copy in small:
        copy.start()
    copies = fetch(m_hbm, buf, sems, 0, near_ref.shape[0])
    for copy in small:
        copy.wait()
    slots = m_hbm.shape[0]
    patterns = gain_ref.shape[0]
    onehot = (ids_ref[...] == iota((patterns, 128), 0)).astype(BF16)
    half_gain[...] = 0.5 * gain_pick(gain_ref[...], onehot)
    wide = jnp.broadcast_to(pos_ref[...].astype(F32), (128, slots)).astype(BF16)
    slot, row = iota((4 * slots, slots), 1), iota((4 * slots, slots), 0)
    map_ref[...] = dot((slot == 2 * (row >> 3) + ((row >> 1) & 1)).astype(BF16), wide, ((1,), (1,)))
    slot, row = iota((2 * slots, slots), 1), iota((2 * slots, slots), 0)
    note_ref[...] = dot((slot == 2 * (row >> 2) + (row & 1)).astype(BF16), wide, ((1,), (1,)))
    for c in range(len(copies)):
        arrive(copies, c)
        build(buf, near_ref, half_gain, 2 * c)


def gain_pick(gain, onehot):
    dims = ((0,), (0,))
    high = gain.astype(BF16)
    rest = gain - high.astype(F32)
    middle = rest.astype(BF16)
    low = (rest - middle.astype(F32)).astype(BF16)
    return dot(high, onehot, dims) + (dot(middle, onehot, dims) + dot(low, onehot, dims))


def tiles(*refs):
    return [ref.at[t] for ref in refs for t in range(ref.shape[0])]


def pull(rows, cov):
    total = 0.0
    for x, tile in zip(rows, cov):
        first = (iota(x.shape, 0) & 1) == 0
        left = jnp.concatenate([jnp.where(first, x, 0.0), jnp.where(first, 0.0, x)], axis=1)
        total = total + dot(left.astype(BF16), tile[...])
    return total


def own_columns(total, kind):
    rows = total[4 * kind : 4 * kind + 4]
    own = jnp.where(iota((4, 128), 0) < 2, rows[:, :128], rows[:, 128:])
    return jnp.sum(own, axis=0, keepdims=True)


def push(row, plain, cov, out_ref):
    spot = iota((8, 128), 0)
    value = jnp.broadcast_to(row, (8, 128))
    if plain:
        value = jnp.where(spot < 4, 1.0, value)
    own = (spot & 2) == 0
    left = jnp.concatenate([jnp.where(own, value, 0.0), jnp.where(own, 0.0, value)], axis=1).astype(BF16)
    first = (spot & 1) == 0
    held = None
    for t, tile in enumerate(cov):
        product = dot(left, tile[...], ((1,), (1,)))
        rows = jnp.where(first, product[:, :128], product[:, 128:])
        if plain:
            out_ref[t * 8 : (t + 1) * 8, :] = rows
        elif t % 2 == 0:
            held = rows
        else:
            out_ref[t * 4 - 4 : t * 4 + 4, :] = jnp.where(spot < 4, held, rows)


def first_pull_kernel(ag_ref, map_ref, note_ref, half_gain, near_ref, m_hbm, out_ref, far_ref, pick_ref, buf, sems):
    rows = map_ref.shape[0]
    near, pairs = near_ref.shape[0], ag_ref.shape[0]
    copies = fetch(m_hbm, buf, sems, near, pairs)
    marks = map_ref[...]
    row = iota((rows, 128), 0)
    key = jnp.where((marks >= 0.0) & ((row & 4) == 0), marks * 2.0 + (row & 1).astype(F32), -1.0)
    pick_ref[...] = (iota((rows, 128), 1).astype(F32) == key).astype(F32)
    plain = iota((8, 128), 0) >= 4

    def message_rows(t):
        part = slice(t * 8, (t + 1) * 8)
        picked = dot(pick_ref[part, :32].astype(BF16), ag_ref[t])
        return jnp.where(plain, (map_ref[part, :] >= 0.0).astype(F32), picked)

    total = pull([message_rows(t) for t in range(near)], tiles(near_ref))
    late = [message_rows(t) for t in range(near, pairs)]
    far = tiles(far_ref)
    for c in range(len(copies)):
        arrive(copies, c)
        build(buf, far_ref, half_gain, 2 * c)
        part = slice(2 * c, 2 * c + 2)
        total = total + pull(late[part], far[part])
    sums, pulled = own_columns(total, 1), own_columns(total, 0)
    place = iota(out_ref.shape, 0) & 3
    out_ref[...] = jnp.where(place == 0, sums, jnp.where(place == 1, pulled, note_ref[...]))


def first_push_kernel(in_ref, price_ref, site_ref, near_ref, far_ref, out_ref, new_ref, sum_ref):
    totals = jnp.sum(in_ref[...].reshape(-1, 8, 128), axis=0)
    column_sum = totals[0:1] + totals[4:5]
    pulled = totals[1:2] + totals[5:6]
    new = jnp.clip(site_ref[...] - (price_ref[...] - pulled / column_sum), 0.0, 1.0)
    new_ref[...] = new
    sum_ref[...] = column_sum
    push(2.0 * new - site_ref[...], True, tiles(near_ref, far_ref), out_ref)


def first_spread_kernel(x_ref, note_ref, out_ref, key_ref):
    notes = note_ref[...].astype(BF16)
    peers = notes.shape[0]

    def positions(rows, shift):
        row, column = iota((rows, peers), 0), iota((rows, peers), 1)
        return dot((column == 4 * (row >> shift) + 2 + ((row >> 1) & 1)).astype(BF16), notes)

    rows = x_ref.shape[0]
    row = iota((rows, 128), 0)
    marks = positions(rows, 3)
    key = jnp.where(marks >= 0.0, ((row >> 2) & 1).astype(F32) * 32.0 + marks * 2.0 + (row & 1).astype(F32), -1.0)
    onehot = (iota((rows, 128), 1).astype(F32) == key).astype(BF16)[:, :64]
    spread = exact_pick(onehot, x_ref[...], ((0,), (0,)))
    for s in range(out_ref.shape[0]):
        out_ref[s] = spread
    row = iota(key_ref.shape, 0)
    marks = positions(key_ref.shape[0], 2)
    key_ref[...] = jnp.where(marks >= 0.0, marks * 2.0 + (row & 1).astype(F32), -1.0)


def chooser(key_ref):
    return (iota(key_ref.shape, 1).astype(F32) == key_ref[...]).astype(BF16)[:, :32]


def step(pixel, dual, weight, pushed, row_sum):
    new = jnp.clip(pixel - (dual - weight), 0.0, 1.0)
    return new, jnp.maximum(dual + ((2.0 * new - pixel) - pushed) / (row_sum + 1.0), 0.0)


def first_dual_kernel(in_ref, key_ref, dual_ref, weight_ref, pixel_ref, out_ref, new_dual_ref, new_pixel_ref, row_ref):
    totals = jnp.sum(in_ref[...], axis=0)
    row_sum = totals[:32]
    row_ref[...] = row_sum
    new_pixel, new_dual = step(pixel_ref[...], dual_ref[...], weight_ref[...], totals[32:], row_sum)
    new_pixel_ref[...] = new_pixel
    new_dual_ref[...] = new_dual
    out_ref[...] = dot(chooser(key_ref), new_dual.astype(BF16))


def pull_kernel(x_ref, near_ref, far_ref, out_ref):
    cov = tiles(near_ref, far_ref)
    total = pull([x_ref[t * 4 : (t + 1) * 4, :] for t in range(len(cov))], cov)
    out_ref[...] = jnp.broadcast_to(own_columns(total, 0), out_ref.shape)


def push_kernel(in_ref, price_ref, site_ref, sum_ref, near_ref, far_ref, out_ref, new_ref):
    pulled = jnp.sum(in_ref[...], axis=0, keepdims=True)
    new = jnp.clip(site_ref[...] - (price_ref[...] - pulled / sum_ref[...]), 0.0, 1.0)
    new_ref[...] = new
    push(2.0 * new - site_ref[...], False, tiles(near_ref, far_ref), out_ref)


def spread_kernel(x_ref, key_ref, out_ref):
    spread = exact_pick(chooser(key_ref), x_ref[...], ((0,), (0,)))
    for s in range(out_ref.shape[0]):
        out_ref[s] = spread


def dual_kernel(in_ref, row_ref, dual_ref, weight_ref, pixel_ref, new_dual_ref, new_pixel_ref):
    pushed = jnp.sum(in_ref[...], axis=0)
    new_pixel_ref[...], new_dual_ref[...] = step(
        pixel_ref[...], dual_ref[...], weight_ref[...], pushed, row_ref[...]
    )


def local(
    n_pix,
    n_site,
    margins,
    block_pos,
    pattern_ids,
    pattern_gain,
    site_price,
    weights,
    site_start,
    pixel_start,
    dual_start,
):
    slots = margins.shape[0]
    rows = 4 * slots
    to_pix = lambda x: lax.all_to_all(x.reshape(n_pix, -1, 128), "pix", 0, 0, tiled=True).reshape(-1, 128)
    to_site = lambda x: lax.all_to_all(x, "site", 0, 0, tiled=True)
    price, site0 = site_price.reshape(1, 128), site_start.reshape(1, 128)
    dual0, weight, pixel0 = (v.reshape(32, 128) for v in (dual_start, weights, pixel_start))

    pairs, near = slots // 2, slots * 11 // 32 // 2 * 2
    far = pairs - near
    (copies,) = call(
        prepare_kernel,
        [((n_pix, 32, 128), BF16)],
        in_hbm(dual0),
        scratch=[pltpu.VMEM((32, 128), F32), pltpu.SemaphoreType.DMA],
        specs=[HBM],
    )
    gathered = to_pix(copies).reshape(n_pix, 32, 128)
    near_tiles, marks, notes, half_gain = call(
        build_kernel,
        [((near, 256, 256), BF16), ((4 * slots, 128), F32), ((2 * slots, 128), F32), ((256, 128), F32)],
        *(in_hbm(v) for v in (margins, block_pos.reshape(1, slots), pattern_ids.reshape(1, 128), pattern_gain)),
        scratch=[
            pltpu.VMEM((2 * near, 256, 128), jnp.int32),
            pltpu.VMEM((1, slots), jnp.int32),
            pltpu.VMEM((1, 128), jnp.int32),
            pltpu.VMEM(pattern_gain.shape, F32),
            pltpu.SemaphoreType.DMA((near // 2,)),
            pltpu.SemaphoreType.DMA((3,)),
        ],
        specs=[HBM] * 4,
        flops=10 * margins.size,
        nbytes=6 * margins.size,
        mib=16,
    )
    message, half_message, line, vector = [((n, 128), F32) for n in (4 * slots, 2 * slots, 1, 32)]
    out, far_tiles = call(
        first_pull_kernel,
        [half_message, ((far, 256, 256), BF16)],
        gathered,
        marks,
        notes,
        half_gain,
        near_tiles,
        in_hbm(margins),
        scratch=[
            pltpu.VMEM((4 * slots, 128), F32),
            pltpu.VMEM((2 * far, 256, 128), jnp.int32),
            pltpu.SemaphoreType.DMA((far // 2,)),
        ],
        specs=[VMEM] * 5 + [HBM],
    )
    cov = (near_tiles, far_tiles)
    summed = to_pix(out)
    out, site1, column_sum = call(first_push_kernel, [message, line, line], summed, price, site0, *cov)
    out, key = call(first_spread_kernel, [((n_site, 64, 128), F32), half_message], to_pix(out), summed)
    out, dual1, pixel1, row_sum = call(
        first_dual_kernel, [half_message] + [vector] * 3, to_site(out), key, dual0, weight, pixel0
    )
    (out,) = call(pull_kernel, [((n_pix, 128), F32)], to_pix(out), *cov)
    out, site2 = call(push_kernel, [half_message, line], to_pix(out), price, site1, column_sum, *cov)
    (out,) = call(spread_kernel, [((n_site, 32, 128), F32)], to_pix(out), key)
    dual2, pixel2 = call(dual_kernel, [vector] * 2, to_site(out), row_sum, dual1, weight, pixel1)
    return site2.reshape(-1), pixel2.reshape(-1), dual2.reshape(-1)


def solution(mesh):
    placed = (
        P("pix", None, "site"),
        P("pix", "site"),
        P("site"),
        P(),
        P("site"),
        P("pix"),
        P("site"),
        P("pix"),
        P("pix"),
    )
    return jax.shard_map(
        functools.partial(local, mesh.shape["pix"], mesh.shape["site"]),
        mesh=mesh,
        in_specs=placed,
        out_specs=(P("site"), P("pix"), P("pix")),
        check_vma=False,
    )
```

time: 115 us -> 113 us (0.983)
  waiting for transfers between devices: 2.12 us -> 5.02 us
  blocking collectives: 88.6 us -> 85.7 us
  Pallas kernels: 14.8 us -> 12.2 us
    all_to_all x5, blocking collectives: 59 us -> 56 us  [local(): lax.all_to_all(x.reshape(n_pix, -1, 128), 'pix', 0, 0, tiled=True)]
    all_to_all x1, waiting for transfers between devices: 2.12 us -> 5.02 us  [local(): lax.all_to_all(x.reshape(n_pix, -1, 128), 'pix', 0, 0, tiled=True)]
    pallas_call x10, Pallas kernels: 14.8 us -> 12.2 us  [call(): pl.pallas_call(body, out_shape=[jax.ShapeDtypeStruct(*o) for o in outs],...]
  transfers between devices with their start and end apart: 1 -> 1, of which waited for: 1 -> 1; matrix products, arithmetic and copies ran while one was open for 0% -> 0% of each run, Pallas kernels for 6% -> 3%
where the time goes in v3:
time: 113 us; the launch traced here: 112 us
  blocking collectives  85.7 us (76%)
  Pallas kernels  12.2 us (11%)
  starting transfers between devices  8.59 us (8%)
  waiting for transfers between devices  5.02 us (4%)
    all_to_all x5, blocking collectives, local(): lax.all_to_all(x.reshape(n_pix, -1, 128), 'pix', 0, 0, tiled=True)  56 us
    all_to_all x2, blocking collectives, local(): to_site = lambda x: lax.all_to_all(x, 'site', 0, 0, tiled=True)  29.7 us
    pallas_call x10, Pallas kernels, call(): pl.pallas_call(body, out_shape=[jax.ShapeDtypeStruct(*o) for o in outs],...  12.2 us
    all_to_all x1, starting transfers between devices, local(): lax.all_to_all(x.reshape(n_pix, -1, 128), 'pix', 0, 0, tiled=True)  8.59 us
    all_to_all x1, waiting for transfers between devices, local(): lax.all_to_all(x.reshape(n_pix, -1, 128), 'pix', 0, 0, tiled=True)  5.02 us
  transfers between devices with their start and end apart: 1, of which 1 were waited for; matrix products, arithmetic and copies ran while one was open for 0% of the time, Pallas kernels for 3%

profile of v3, /device:TPU:1, one launch (start us, length us, event | category | flops | bytes accessed | tf_op | source)
XLA Modules:
  0.0 112.2 jit_solution(8013544766968377151)
XLA Ops:
  0.6 1.4 %shard_map.112 = bf16[32,32,128]{2,1,0:T(8,128)(2,1)} custom-call(f32[32,128]{1,0:T(8,128)} %bitcast.30), custom_call_target="tpu_custom_call" | custom-call | tf_op jit(solution)/shard_map/pallas_call | solution.py:34
  2.1 8.6 %all-to-all-start = ((bf16[32,32,128]{2,1,0:T(8,128)(2,1)}), bf16[32,32,128]{2,1,0:T(8,128)(2,1)S(1)}, u32[]{:S(2)}, u32[]{:S(2)}) async-start(bf16[32,32,128]{2,1,0:T(8,128)(2,1)} %shard_map.112), calls=%async_computation | async-start | bytes 524288 | tf_op jit(solution)/shard_map/all_to_all | solution.py:292
  10.7 3.8 %shard_map.113 = (bf16[22,256,256]{2,1,0:T(8,128)(2,1)S(1)}, f32[256,128]{1,0:T(8,128)S(1)}, f32[128,128]{1,0:T(8,128)S(1)}, f32[256,128]{1,0:T(8,128)S(1)}) custom-call(s32[64,256,128]{2,1,0:T(8,128)} %m_hbm.3, s32[1,64]{1,0:T(1,128)} %bitcast.41, s32[1,128]{1,0:T(1,128)} %bitcast.42, f32[16,256]{1,0:T(8,128)} %gain_hbm.1), custom_call_target="tpu_custom_call" | custom-call | flops 20971520 | bytes 12582912 | tf_op jit(solution)/shard_map/pallas_call | solution.py:34
  14.5 5.0 %all-to-all-done.ag_ref = bf16[32,32,128]{2,1,0:T(8,128)(2,1)S(1)} async-done(((bf16[32,32,128]{2,1,0:T(8,128)(2,1)}), bf16[32,32,128]{2,1,0:T(8,128)(2,1)S(1)}, u32[]{:S(2)}, u32[]{:S(2)}) %all-to-all-start) | async-done | bytes 262176 | tf_op jit(solution)/shard_map/all_to_all | solution.py:292
  19.5 0.0 copy-start.3
  19.5 0.0 copy-start.4
  19.6 2.1 %shard_map.114 = (f32[128,128]{1,0:T(8,128)S(1)}, bf16[10,256,256]{2,1,0:T(8,128)(2,1)S(1)}) custom-call(bf16[32,32,128]{2,1,0:T(8,128)(2,1)S(1)} %all-to-all-done.ag_ref, f32[256,128]{1,0:T(8,128)S(1)} %get-tuple-element.22.map_ref, f32[128,128]{1,0:T(8,128)S(1)} %get-tuple-element.23.note_ref, f32[256,128]{1,0:T(8,128)S(1)} %get-tuple-element.24.half_gain, ...), custom_call_target="tpu_custom_call" | custom-call | tf_op jit(solution)/shard_map/pallas_call | solution.py:34
  21.7 0.0 copy-start
  21.7 0.0 copy-start.1
  21.7 0.0 copy-start.2
  21.7 11.0 %all_to_all.40 = f32[32,4,128]{2,1,0:T(4,128)S(1)} all-to-all(f32[32,4,128]{2,1,0:T(4,128)S(1)} %bitcast.35), channel_id=1, replica_groups=mesh['pix'=32,'site'=8] {'pix'}, dimensions={0} | all-to-all | bytes 131072 | tf_op jit(solution)/shard_map/all_to_all | solution.py:292
  32.7 0.0 copy-done.3
  32.7 0.0 copy-done.4
  32.7 1.2 %shard_map.115 = (f32[256,128]{1,0:T(8,128)S(1)}, f32[1,128]{1,0:T(1,128)S(1)}, f32[1,128]{1,0:T(1,128)S(1)}) custom-call(f32[128,128]{1,0:T(8,128)S(1)} %bitcast.22, f32[1,128]{1,0:T(1,128)S(1)} %bitcast.38, f32[1,128]{1,0:T(1,128)S(1)} %bitcast.40, bf16[22,256,256]{2,1,0:T(8,128)(2,1)S(1)} %get-tuple-element.25.near_ref, ...), custom_call_target="tpu_custom_call" | custom-call | tf_op jit(solution)/shard_map/pallas_call | solution.py:34
  33.9 11.2 %all_to_all.41 = f32[32,8,128]{2,1,0:T(8,128)S(1)} all-to-all(f32[32,8,128]{2,1,0:T(8,128)S(1)} %bitcast.27), channel_id=1, replica_groups=mesh['pix'=32,'site'=8] {'pix'}, dimensions={0} | all-to-all | bytes 262144 | tf_op jit(solution)/shard_map/all_to_all | solution.py:292
  45.1 0.4 shard_map.116
  45.5 19.0 %all_to_all.42.in_ref = f32[8,64,128]{2,1,0:T(8,128)S(1)} all-to-all(f32[8,64,128]{2,1,0:T(8,128)S(1)} %get-tuple-element.29), channel_id=1, replica_groups=mesh['pix'=32,'site'=8] {'site'}, dimensions={0} | all-to-all | bytes 524288 | tf_op jit(solution)/shard_map/all_to_all | solution.py:293
  64.5 0.0 copy-done
  64.5 0.0 copy-done.1
  64.5 0.0 copy-done.2
  64.5 0.1 shard_map.117
  64.6 12.3 %all_to_all.43 = f32[32,4,128]{2,1,0:T(4,128)S(1)} all-to-all(f32[32,4,128]{2,1,0:T(4,128)S(1)} %bitcast.36), channel_id=1, replica_groups=mesh['pix'=32,'site'=8] {'pix'}, dimensions={0} | all-to-all | bytes 131072 | tf_op jit(solution)/shard_map/all_to_all | solution.py:292
  76.9 0.7 shard_map.118
  77.6 10.5 %all_to_all.44 = f32[32,1,128]{2,1,0:T(1,128)S(1)} all-to-all(f32[32,1,128]{2,1,0:T(1,128)S(1)} %bitcast.29), channel_id=1, replica_groups=mesh['pix'=32,'site'=8] {'pix'}, dimensions={0} | all-to-all | bytes 32768 | tf_op jit(solution)/shard_map/all_to_all | solution.py:292
  88.1 1.5 %shard_map.119 = (f32[128,128]{1,0:T(8,128)S(1)}, f32[1,128]{1,0:T(1,128)}) custom-call(f32[32,128]{1,0:T(8,128)S(1)} %bitcast.28, f32[1,128]{1,0:T(1,128)S(1)} %bitcast.39, f32[1,128]{1,0:T(1,128)S(1)} %get-tuple-element.32.site_ref, f32[1,128]{1,0:T(1,128)S(1)} %get-tuple-element.33.sum_ref, bf16[22,256,256]{2,1,0:T(8,128)(2,1)S(1)} %get-tuple-element.25.near_ref, ...), custom_call_target="tpu_custom_call" | custom-call | tf_op jit(solution)/shard_map/pallas_call | solution.py:34
  89.6 11.0 %all_to_all.45 = f32[32,4,128]{2,1,0:T(4,128)S(1)} all-to-all(f32[32,4,128]{2,1,0:T(4,128)S(1)} %bitcast.34), channel_id=1, replica_groups=mesh['pix'=32,'site'=8] {'pix'}, dimensions={0} | all-to-all | bytes 131072 | tf_op jit(solution)/shard_map/all_to_all | solution.py:292
  100.6 0.2 shard_map.120
  100.9 10.7 %all_to_all.46.in_ref = f32[8,32,128]{2,1,0:T(8,128)S(1)} all-to-all(f32[8,32,128]{2,1,0:T(8,128)S(1)} %shard_map.120), channel_id=1, replica_groups=mesh['pix'=32,'site'=8] {'site'}, dimensions={0} | all-to-all | bytes 262144 | tf_op jit(solution)/shard_map/all_to_all | solution.py:293
  111.6 0.6 shard_map.121
Async XLA Ops:
  2.1 17.5 %all-to-all-start = ((bf16[32,32,128]{2,1,0:T(8,128)(2,1)}), bf16[32,32,128]{2,1,0:T(8,128)(2,1)S(1)}, u32[]{:S(2)}, u32[]{:S(2)}) async-start(bf16[32,32,128]{2,1,0:T(8,128)(2,1)} %shard_map.112), calls=%async_computation | async-start | bytes 524288 | tf_op jit(solution)/shard_map/all_to_all | solution.py:292
  19.5 13.2 %copy-start.3 = (f32[128]{0:T(128)S(1)}, f32[128]{0:T(128)}, u32[]{:S(2)}) copy-start(f32[128]{0:T(128)} %param.13) | copy-start | bytes 1540
  19.5 13.2 %copy-start.4 = (f32[128]{0:T(128)S(1)}, f32[128]{0:T(128)}, u32[]{:S(2)}) copy-start(f32[128]{0:T(128)} %param.15) | copy-start | bytes 1540
  21.7 42.8 %copy-start = (f32[4096]{0:T(1024)S(1)}, f32[4096]{0:T(1024)}, u32[]{:S(2)}) copy-start(f32[4096]{0:T(1024)} %param.17) | copy-start | bytes 49156
  21.7 42.7 %copy-start.1 = (f32[4096]{0:T(1024)S(1)}, f32[4096]{0:T(1024)}, u32[]{:S(2)}) copy-start(f32[4096]{0:T(1024)} %param.14) | copy-start | bytes 49156
  21.7 42.7 %copy-start.2 = (f32[4096]{0:T(1024)S(1)}, f32[4096]{0:T(1024)}, u32[]{:S(2)}) copy-start(f32[4096]{0:T(1024)} %param.16) | copy-start | bytes 49156

commit v4 on v3

--- a/solution.py
+++ b/solution.py
@@ -44,15 +44,6 @@
 
 def in_hbm(value):
     return pltpu.with_memory_space_constraint(value, pltpu.HBM)
-
-
-def prepare_kernel(dual_hbm, out_ref, dual_ref, sem):
-    copy = pltpu.make_async_copy(dual_hbm, dual_ref, sem)
-    copy.start()
-    copy.wait()
-    dual = dual_ref[...].astype(BF16)
-    for t in range(out_ref.shape[0]):
-        out_ref[t] = dual
 
 
 AHEAD = 6
@@ -158,16 +149,13 @@
     own = (spot & 2) == 0
     left = jnp.concatenate([jnp.where(own, value, 0.0), jnp.where(own, 0.0, value)], axis=1).astype(BF16)
     first = (spot & 1) == 0
-    held = None
     for t, tile in enumerate(cov):
         product = dot(left, tile[...], ((1,), (1,)))
         rows = jnp.where(first, product[:, :128], product[:, 128:])
         if plain:
             out_ref[t * 8 : (t + 1) * 8, :] = rows
-        elif t % 2 == 0:
-            held = rows
         else:
-            out_ref[t * 4 - 4 : t * 4 + 4, :] = jnp.where(spot < 4, held, rows)
+            out_ref[t * 4 : t * 4 + 4, :] = rows[:4]
 
 
 def first_pull_kernel(ag_ref, map_ref, note_ref, half_gain, near_ref, m_hbm, out_ref, far_ref, pick_ref, buf, sems):
@@ -296,13 +284,8 @@
 
     pairs, near = slots // 2, slots * 11 // 32 // 2 * 2
     far = pairs - near
-    (copies,) = call(
-        prepare_kernel,
-        [((n_pix, 32, 128), BF16)],
-        in_hbm(dual0),
-        scratch=[pltpu.VMEM((32, 128), F32), pltpu.SemaphoreType.DMA],
-        specs=[HBM],
-    )
+    spot = iota((n_pix, 32, 128), 0) + iota((n_pix, 32, 128), 1) + iota((n_pix, 32, 128), 2)
+    copies = jnp.where(spot < n_pix * 4096, dual0[None], 0.0).astype(BF16)
     gathered = to_pix(copies).reshape(n_pix, 32, 128)
     near_tiles, marks, notes, half_gain = call(
         build_kernel,

time: 113 us -> 112 us (level)
  Pallas kernels: 12.2 us -> 10.4 us
  other arithmetic: 0 us -> 1.45 us
    pallas_call x10 -> x9, Pallas kernels: 12.2 us -> 10.4 us  [call(): pl.pallas_call(body, out_shape=[jax.ShapeDtypeStruct(*o) for o in outs],...]
    convert_element_type x0 -> x1, other arithmetic: none -> 1.45 us  [local(): copies = jnp.where(spot < n_pix * 4096, dual0[None], 0.0).astype(BF16)]
where the time goes in v4:
time: 112 us
  blocking collectives  85.7 us (77%)
  Pallas kernels  10.4 us (9%)
  starting transfers between devices  8.58 us (8%)
  waiting for transfers between devices  5.02 us (4%)
  other arithmetic  1.45 us (1%)
    all_to_all x5, blocking collectives, local(): lax.all_to_all(x.reshape(n_pix, -1, 128), 'pix', 0, 0, tiled=True)  56 us
    all_to_all x2, blocking collectives, local(): to_site = lambda x: lax.all_to_all(x, 'site', 0, 0, tiled=True)  29.7 us
    pallas_call x9, Pallas kernels, call(): pl.pallas_call(body, out_shape=[jax.ShapeDtypeStruct(*o) for o in outs],...  10.4 us
    all_to_all x1, starting transfers between devices, local(): lax.all_to_all(x.reshape(n_pix, -1, 128), 'pix', 0, 0, tiled=True)  8.58 us
    all_to_all x1, waiting for transfers between devices, local(): lax.all_to_all(x.reshape(n_pix, -1, 128), 'pix', 0, 0, tiled=True)  5.02 us
  transfers between devices with their start and end apart: 1, of which 1 were waited for; matrix products, arithmetic and copies ran while one was open for 0% of the time, Pallas kernels for 3%

profile of v4, /device:TPU:1, one launch (start us, length us, event | category | flops | bytes accessed | tf_op | source)
XLA Modules:
  0.0 111.8 jit_solution(13973571116593184574)
XLA Ops:
  0.6 1.4 %select_convert_fusion = bf16[32,32,128]{2,1,0:T(8,128)(2,1)} fusion(f32[32,128]{1,0:T(8,128)} %bitcast.30), kind=kLoop, calls=%fused_computation | loop fusion | flops 524288 | bytes 278528 | tf_op jit(solution)/shard_map/convert_element_type | solution.py:288
  2.1 8.6 %all-to-all-start = ((bf16[32,32,128]{2,1,0:T(8,128)(2,1)}), bf16[32,32,128]{2,1,0:T(8,128)(2,1)S(1)}, u32[]{:S(2)}, u32[]{:S(2)}) async-start(bf16[32,32,128]{2,1,0:T(8,128)(2,1)} %select_convert_fusion), calls=%async_computation | async-start | bytes 524288 | tf_op jit(solution)/shard_map/all_to_all | solution.py:280
  10.7 3.8 %shard_map.112 = (bf16[22,256,256]{2,1,0:T(8,128)(2,1)S(1)}, f32[256,128]{1,0:T(8,128)S(1)}, f32[128,128]{1,0:T(8,128)S(1)}, f32[256,128]{1,0:T(8,128)S(1)}) custom-call(s32[64,256,128]{2,1,0:T(8,128)} %m_hbm.3, s32[1,64]{1,0:T(1,128)} %bitcast.41, s32[1,128]{1,0:T(1,128)} %bitcast.42, f32[16,256]{1,0:T(8,128)} %gain_hbm.1), custom_call_target="tpu_custom_call" | custom-call | flops 20971520 | bytes 12582912 | tf_op jit(solution)/shard_map/pallas_call | solution.py:34
  14.5 5.0 %all-to-all-done.ag_ref = bf16[32,32,128]{2,1,0:T(8,128)(2,1)S(1)} async-done(((bf16[32,32,128]{2,1,0:T(8,128)(2,1)}), bf16[32,32,128]{2,1,0:T(8,128)(2,1)S(1)}, u32[]{:S(2)}, u32[]{:S(2)}) %all-to-all-start) | async-done | bytes 262176 | tf_op jit(solution)/shard_map/all_to_all | solution.py:280
  19.5 0.0 copy-start.3
  19.5 0.0 copy-start.4
  19.5 2.1 %shard_map.113 = (f32[128,128]{1,0:T(8,128)S(1)}, bf16[10,256,256]{2,1,0:T(8,128)(2,1)S(1)}) custom-call(bf16[32,32,128]{2,1,0:T(8,128)(2,1)S(1)} %all-to-all-done.ag_ref, f32[256,128]{1,0:T(8,128)S(1)} %get-tuple-element.22.map_ref, f32[128,128]{1,0:T(8,128)S(1)} %get-tuple-element.23.note_ref, f32[256,128]{1,0:T(8,128)S(1)} %get-tuple-element.24.half_gain, ...), custom_call_target="tpu_custom_call" | custom-call | tf_op jit(solution)/shard_map/pallas_call | solution.py:34
  21.7 0.0 copy-start
  21.7 0.0 copy-start.1
  21.7 0.0 copy-start.2
  21.7 11.0 %all_to_all.40 = f32[32,4,128]{2,1,0:T(4,128)S(1)} all-to-all(f32[32,4,128]{2,1,0:T(4,128)S(1)} %bitcast.35), channel_id=1, replica_groups=mesh['pix'=32,'site'=8] {'pix'}, dimensions={0} | all-to-all | bytes 131072 | tf_op jit(solution)/shard_map/all_to_all | solution.py:280
  32.7 0.0 copy-done.3
  32.7 0.0 copy-done.4
  32.7 1.2 %shard_map.114 = (f32[256,128]{1,0:T(8,128)S(1)}, f32[1,128]{1,0:T(1,128)S(1)}, f32[1,128]{1,0:T(1,128)S(1)}) custom-call(f32[128,128]{1,0:T(8,128)S(1)} %bitcast.22, f32[1,128]{1,0:T(1,128)S(1)} %bitcast.38, f32[1,128]{1,0:T(1,128)S(1)} %bitcast.40, bf16[22,256,256]{2,1,0:T(8,128)(2,1)S(1)} %get-tuple-element.25.near_ref, ...), custom_call_target="tpu_custom_call" | custom-call | tf_op jit(solution)/shard_map/pallas_call | solution.py:34
  33.9 11.2 %all_to_all.41 = f32[32,8,128]{2,1,0:T(8,128)S(1)} all-to-all(f32[32,8,128]{2,1,0:T(8,128)S(1)} %bitcast.27), channel_id=1, replica_groups=mesh['pix'=32,'site'=8] {'pix'}, dimensions={0} | all-to-all | bytes 262144 | tf_op jit(solution)/shard_map/all_to_all | solution.py:280
  45.1 0.4 shard_map.115
  45.5 19.0 %all_to_all.42.in_ref = f32[8,64,128]{2,1,0:T(8,128)S(1)} all-to-all(f32[8,64,128]{2,1,0:T(8,128)S(1)} %get-tuple-element.29), channel_id=1, replica_groups=mesh['pix'=32,'site'=8] {'site'}, dimensions={0} | all-to-all | bytes 524288 | tf_op jit(solution)/shard_map/all_to_all | solution.py:281
  64.4 0.0 copy-done
  64.4 0.0 copy-done.1
  64.4 0.0 copy-done.2
  64.4 0.1 shard_map.116
  64.6 12.3 %all_to_all.43 = f32[32,4,128]{2,1,0:T(4,128)S(1)} all-to-all(f32[32,4,128]{2,1,0:T(4,128)S(1)} %bitcast.36), channel_id=1, replica_groups=mesh['pix'=32,'site'=8] {'pix'}, dimensions={0} | all-to-all | bytes 131072 | tf_op jit(solution)/shard_map/all_to_all | solution.py:280
  76.9 0.7 shard_map.117
  77.5 10.5 %all_to_all.44 = f32[32,1,128]{2,1,0:T(1,128)S(1)} all-to-all(f32[32,1,128]{2,1,0:T(1,128)S(1)} %bitcast.29), channel_id=1, replica_groups=mesh['pix'=32,'site'=8] {'pix'}, dimensions={0} | all-to-all | bytes 32768 | tf_op jit(solution)/shard_map/all_to_all | solution.py:280
  88.1 1.2 %shard_map.118 = (f32[128,128]{1,0:T(8,128)S(1)}, f32[1,128]{1,0:T(1,128)}) custom-call(f32[32,128]{1,0:T(8,128)S(1)} %bitcast.28, f32[1,128]{1,0:T(1,128)S(1)} %bitcast.39, f32[1,128]{1,0:T(1,128)S(1)} %get-tuple-element.32.site_ref, f32[1,128]{1,0:T(1,128)S(1)} %get-tuple-element.33.sum_ref, bf16[22,256,256]{2,1,0:T(8,128)(2,1)S(1)} %get-tuple-element.25.near_ref, ...), custom_call_target="tpu_custom_call" | custom-call | tf_op jit(solution)/shard_map/pallas_call | solution.py:34
  89.2 11.1 %all_to_all.45 = f32[32,4,128]{2,1,0:T(4,128)S(1)} all-to-all(f32[32,4,128]{2,1,0:T(4,128)S(1)} %bitcast.34), channel_id=1, replica_groups=mesh['pix'=32,'site'=8] {'pix'}, dimensions={0} | all-to-all | bytes 131072 | tf_op jit(solution)/shard_map/all_to_all | solution.py:280
  100.3 0.2 shard_map.119
  100.5 10.7 %all_to_all.46.in_ref = f32[8,32,128]{2,1,0:T(8,128)S(1)} all-to-all(f32[8,32,128]{2,1,0:T(8,128)S(1)} %shard_map.119), channel_id=1, replica_groups=mesh['pix'=32,'site'=8] {'site'}, dimensions={0} | all-to-all | bytes 262144 | tf_op jit(solution)/shard_map/all_to_all | solution.py:281
  111.2 0.6 shard_map.120
Async XLA Ops:
  2.1 17.5 %all-to-all-start = ((bf16[32,32,128]{2,1,0:T(8,128)(2,1)}), bf16[32,32,128]{2,1,0:T(8,128)(2,1)S(1)}, u32[]{:S(2)}, u32[]{:S(2)}) async-start(bf16[32,32,128]{2,1,0:T(8,128)(2,1)} %select_convert_fusion), calls=%async_computation | async-start | bytes 524288 | tf_op jit(solution)/shard_map/all_to_all | solution.py:280
  19.5 13.2 %copy-start.3 = (f32[128]{0:T(128)S(1)}, f32[128]{0:T(128)}, u32[]{:S(2)}) copy-start(f32[128]{0:T(128)} %param.13) | copy-start | bytes 1540
  19.5 13.2 %copy-start.4 = (f32[128]{0:T(128)S(1)}, f32[128]{0:T(128)}, u32[]{:S(2)}) copy-start(f32[128]{0:T(128)} %param.15) | copy-start | bytes 1540
  21.7 42.8 %copy-start = (f32[4096]{0:T(1024)S(1)}, f32[4096]{0:T(1024)}, u32[]{:S(2)}) copy-start(f32[4096]{0:T(1024)} %param.17) | copy-start | bytes 49156
  21.7 42.7 %copy-start.1 = (f32[4096]{0:T(1024)S(1)}, f32[4096]{0:T(1024)}, u32[]{:S(2)}) copy-start(f32[4096]{0:T(1024)} %param.14) | copy-start | bytes 49156
  21.7 42.7 %copy-start.2 = (f32[4096]{0:T(1024)S(1)}, f32[4096]{0:T(1024)}, u32[]{:S(2)}) copy-start(f32[4096]{0:T(1024)} %param.16) | copy-start | bytes 49156

commit v5 on v4

--- a/solution.py
+++ b/solution.py
@@ -47,12 +47,15 @@
 
 
 AHEAD = 6
+LEAD = 20
+SITE_LEAD = 4
 
 
 def fetch(m_hbm, buf, sems, first, last):
     copies = []
-    for c, t in enumerate(range(first, last, 2)):
-        part = (m_hbm.at[pl.ds(2 * t, 4)], buf.at[pl.ds(2 * (t - first), 4)])
+    pairs = m_hbm.shape[0] // 2
+    for c, j in enumerate(range(first, last, 2)):
+        part = (m_hbm.at[pl.ds(2 * ((j + LEAD) % pairs), 4)], buf.at[pl.ds(2 * (j - first), 4)])
         copies.append(pltpu.make_async_copy(*part, sems.at[c]))
     for copy in copies[:AHEAD]:
         copy.start()
@@ -104,10 +107,14 @@
     onehot = (ids_ref[...] == iota((patterns, 128), 0)).astype(BF16)
     half_gain[...] = 0.5 * gain_pick(gain_ref[...], onehot)
     wide = jnp.broadcast_to(pos_ref[...].astype(F32), (128, slots)).astype(BF16)
+
+    def peer(j):
+        return jnp.where(j + LEAD < slots // 2, j + LEAD, j + LEAD - slots // 2)
+
     slot, row = iota((4 * slots, slots), 1), iota((4 * slots, slots), 0)
-    map_ref[...] = dot((slot == 2 * (row >> 3) + ((row >> 1) & 1)).astype(BF16), wide, ((1,), (1,)))
+    map_ref[...] = dot((slot == 2 * peer(row >> 3) + ((row >> 1) & 1)).astype(BF16), wide, ((1,), (1,)))
     slot, row = iota((2 * slots, slots), 1), iota((2 * slots, slots), 0)
-    note_ref[...] = dot((slot == 2 * (row >> 2) + (row & 1)).astype(BF16), wide, ((1,), (1,)))
+    note_ref[...] = dot((slot == 2 * peer(row >> 2) + (row & 1)).astype(BF16), wide, ((1,), (1,)))
     for c in range(len(copies)):
         arrive(copies, c)
         build(buf, near_ref, half_gain, 2 * c)
@@ -277,8 +284,16 @@
 ):
     slots = margins.shape[0]
     rows = 4 * slots
-    to_pix = lambda x: lax.all_to_all(x.reshape(n_pix, -1, 128), "pix", 0, 0, tiled=True).reshape(-1, 128)
-    to_site = lambda x: lax.all_to_all(x, "site", 0, 0, tiled=True)
+    pix_order = [[(j + LEAD) % n_pix for j in range(n_pix)]]
+    site_order = [[(j + SITE_LEAD) % n_site for j in range(n_site)]]
+
+    def to_pix(x):
+        x = x.reshape(n_pix, -1, 128)
+        return lax.all_to_all(x, "pix", 0, 0, tiled=True, axis_index_groups=pix_order).reshape(-1, 128)
+
+    def to_site(x):
+        return lax.all_to_all(x, "site", 0, 0, tiled=True, axis_index_groups=site_order)
+
     price, site0 = site_price.reshape(1, 128), site_start.reshape(1, 128)
     dual0, weight, pixel0 = (v.reshape(32, 128) for v in (dual_start, weights, pixel_start))
 

time: 112 us -> 105 us (0.938)
  waiting for transfers between devices: 5.02 us -> 0.25 us
  blocking collectives: 85.7 us -> 81.4 us
  starting transfers between devices: 8.58 us -> 10.4 us
    all_to_all x1, waiting for transfers between devices: 5.02 us -> 0.25 us  [to_pix(): lax.all_to_all(x, 'pix', 0, 0, tiled=True, axis_index_groups=pix_order)]
    all_to_all x7, blocking collectives: 85.7 us -> 81.4 us  [the longest x5 54.1 us: to_pix(): lax.all_to_all(x, 'pix', 0, 0, tiled=True, axis_index_groups=pix_order)]
    all_to_all x1, starting transfers between devices: 8.58 us -> 10.4 us  [to_pix(): lax.all_to_all(x, 'pix', 0, 0, tiled=True, axis_index_groups=pix_order)]
  transfers between devices with their start and end apart: 1 -> 1, of which waited for: 1 -> 1; matrix products, arithmetic and copies ran while one was open for 0% -> 0% of each run, Pallas kernels for 3% -> 4%
where the time goes in v5:
time: 105 us
  blocking collectives  81.4 us (78%)
  starting transfers between devices  10.4 us (10%)
  Pallas kernels  10.4 us (10%)
  other arithmetic  1.45 us (1%)
    all_to_all x5, blocking collectives, to_pix(): lax.all_to_all(x, 'pix', 0, 0, tiled=True, axis_index_groups=pix_order)  54.1 us
    all_to_all x2, blocking collectives, to_site(): lax.all_to_all(x, 'site', 0, 0, tiled=True, axis_index_groups=site_order)  27.4 us
    pallas_call x9, Pallas kernels, call(): pl.pallas_call(body, out_shape=[jax.ShapeDtypeStruct(*o) for o in outs],...  10.4 us
    all_to_all x1, starting transfers between devices, to_pix(): lax.all_to_all(x, 'pix', 0, 0, tiled=True, axis_index_groups=pix_order)  10.4 us
  transfers between devices with their start and end apart: 1, of which 1 were waited for; matrix products, arithmetic and copies ran while one was open for 0% of the time, Pallas kernels for 4%

profile of v5, /device:TPU:1, one launch (start us, length us, event | category | flops | bytes accessed | tf_op | source)
XLA Modules:
  0.0 104.6 jit_solution(8501710259774303547)
XLA Ops:
  0.6 1.4 %select_convert_fusion = bf16[32,32,128]{2,1,0:T(8,128)(2,1)} fusion(f32[32,128]{1,0:T(8,128)} %bitcast.30), kind=kLoop, calls=%fused_computation | loop fusion | flops 524288 | bytes 278528 | tf_op jit(solution)/shard_map/convert_element_type | solution.py:303
  2.1 10.4 %all-to-all-start = ((bf16[32,32,128]{2,1,0:T(8,128)(2,1)}), bf16[32,32,128]{2,1,0:T(8,128)(2,1)S(1)}, u32[]{:S(2)}, u32[]{:S(2)}) async-start(bf16[32,32,128]{2,1,0:T(8,128)(2,1)} %select_convert_fusion), calls=%async_computation | async-start | bytes 524288 | tf_op jit(solution)/shard_map/all_to_all | solution.py:292
  12.4 3.8 %shard_map.112 = (bf16[22,256,256]{2,1,0:T(8,128)(2,1)S(1)}, f32[256,128]{1,0:T(8,128)S(1)}, f32[128,128]{1,0:T(8,128)S(1)}, f32[256,128]{1,0:T(8,128)S(1)}) custom-call(s32[64,256,128]{2,1,0:T(8,128)} %m_hbm.3, s32[1,64]{1,0:T(1,128)} %bitcast.41, s32[1,128]{1,0:T(1,128)} %bitcast.42, f32[16,256]{1,0:T(8,128)} %gain_hbm.1), custom_call_target="tpu_custom_call" | custom-call | flops 20971520 | bytes 12582912 | tf_op jit(solution)/shard_map/pallas_call | solution.py:34
  16.3 0.3 all-to-all-done.ag_ref
  16.5 0.0 copy-start.3
  16.6 0.0 copy-start.4
  16.6 2.1 %shard_map.113 = (f32[128,128]{1,0:T(8,128)S(1)}, bf16[10,256,256]{2,1,0:T(8,128)(2,1)S(1)}) custom-call(bf16[32,32,128]{2,1,0:T(8,128)(2,1)S(1)} %all-to-all-done.ag_ref, f32[256,128]{1,0:T(8,128)S(1)} %get-tuple-element.22.map_ref, f32[128,128]{1,0:T(8,128)S(1)} %get-tuple-element.23.note_ref, f32[256,128]{1,0:T(8,128)S(1)} %get-tuple-element.24.half_gain, ...), custom_call_target="tpu_custom_call" | custom-call | tf_op jit(solution)/shard_map/pallas_call | solution.py:34
  18.7 0.0 copy-start
  18.7 0.0 copy-start.1
  18.7 0.0 copy-start.2
  18.7 10.4 %all_to_all.40 = f32[32,4,128]{2,1,0:T(4,128)S(1)} all-to-all(f32[32,4,128]{2,1,0:T(4,128)S(1)} %bitcast.35), channel_id=1, replica_groups={{160,168,176,184,192,200,208,216,224,232,240,248,0,8,16,24,32,40,48,56,..., dimensions={0} | all-to-all | bytes 131072 | tf_op jit(solution)/shard_map/all_to_all | solution.py:292
  29.2 0.0 copy-done.3
  29.2 0.0 copy-done.4
  29.2 1.2 %shard_map.114 = (f32[256,128]{1,0:T(8,128)S(1)}, f32[1,128]{1,0:T(1,128)S(1)}, f32[1,128]{1,0:T(1,128)S(1)}) custom-call(f32[128,128]{1,0:T(8,128)S(1)} %bitcast.22, f32[1,128]{1,0:T(1,128)S(1)} %bitcast.38, f32[1,128]{1,0:T(1,128)S(1)} %bitcast.40, bf16[22,256,256]{2,1,0:T(8,128)(2,1)S(1)} %get-tuple-element.25.near_ref, ...), custom_call_target="tpu_custom_call" | custom-call | tf_op jit(solution)/shard_map/pallas_call | solution.py:34
  30.4 11.0 %all_to_all.41 = f32[32,8,128]{2,1,0:T(8,128)S(1)} all-to-all(f32[32,8,128]{2,1,0:T(8,128)S(1)} %bitcast.27), channel_id=1, replica_groups={{160,168,176,184,192,200,208,216,224,232,240,248,0,8,16,24,32,40,48,56,..., dimensions={0} | all-to-all | bytes 262144 | tf_op jit(solution)/shard_map/all_to_all | solution.py:292
  41.4 0.4 shard_map.115
  41.8 16.2 %all_to_all.42.in_ref = f32[8,64,128]{2,1,0:T(8,128)S(1)} all-to-all(f32[8,64,128]{2,1,0:T(8,128)S(1)} %get-tuple-element.29), channel_id=1, replica_groups={{4,5,6,7,0,1,2,3},{12,13,14,15,8,9,10,11},{20,21,22,23,16,17,18,19},{28..., dimensions={0} | all-to-all | bytes 524288 | tf_op jit(solution)/shard_map/all_to_all | solution.py:295
  58.0 0.0 copy-done
  58.0 0.0 copy-done.1
  58.0 0.0 copy-done.2
  58.0 0.1 shard_map.116
  58.1 11.3 %all_to_all.43 = f32[32,4,128]{2,1,0:T(4,128)S(1)} all-to-all(f32[32,4,128]{2,1,0:T(4,128)S(1)} %bitcast.36), channel_id=1, replica_groups={{160,168,176,184,192,200,208,216,224,232,240,248,0,8,16,24,32,40,48,56,..., dimensions={0} | all-to-all | bytes 131072 | tf_op jit(solution)/shard_map/all_to_all | solution.py:292
  69.5 0.7 shard_map.117
  70.1 10.3 %all_to_all.44 = f32[32,1,128]{2,1,0:T(1,128)S(1)} all-to-all(f32[32,1,128]{2,1,0:T(1,128)S(1)} %bitcast.29), channel_id=1, replica_groups={{160,168,176,184,192,200,208,216,224,232,240,248,0,8,16,24,32,40,48,56,..., dimensions={0} | all-to-all | bytes 32768 | tf_op jit(solution)/shard_map/all_to_all | solution.py:292
  80.4 1.2 %shard_map.118 = (f32[128,128]{1,0:T(8,128)S(1)}, f32[1,128]{1,0:T(1,128)}) custom-call(f32[32,128]{1,0:T(8,128)S(1)} %bitcast.28, f32[1,128]{1,0:T(1,128)S(1)} %bitcast.39, f32[1,128]{1,0:T(1,128)S(1)} %get-tuple-element.32.site_ref, f32[1,128]{1,0:T(1,128)S(1)} %get-tuple-element.33.sum_ref, bf16[22,256,256]{2,1,0:T(8,128)(2,1)S(1)} %get-tuple-element.25.near_ref, ...), custom_call_target="tpu_custom_call" | custom-call | tf_op jit(solution)/shard_map/pallas_call | solution.py:34
  81.6 11.0 %all_to_all.45 = f32[32,4,128]{2,1,0:T(4,128)S(1)} all-to-all(f32[32,4,128]{2,1,0:T(4,128)S(1)} %bitcast.34), channel_id=1, replica_groups={{160,168,176,184,192,200,208,216,224,232,240,248,0,8,16,24,32,40,48,56,..., dimensions={0} | all-to-all | bytes 131072 | tf_op jit(solution)/shard_map/all_to_all | solution.py:292
  92.6 0.2 shard_map.119
  92.8 11.2 %all_to_all.46.in_ref = f32[8,32,128]{2,1,0:T(8,128)S(1)} all-to-all(f32[8,32,128]{2,1,0:T(8,128)S(1)} %shard_map.119), channel_id=1, replica_groups={{4,5,6,7,0,1,2,3},{12,13,14,15,8,9,10,11},{20,21,22,23,16,17,18,19},{28..., dimensions={0} | all-to-all | bytes 262144 | tf_op jit(solution)/shard_map/all_to_all | solution.py:295
  104.0 0.6 shard_map.120
Async XLA Ops:
  2.1 14.5 %all-to-all-start = ((bf16[32,32,128]{2,1,0:T(8,128)(2,1)}), bf16[32,32,128]{2,1,0:T(8,128)(2,1)S(1)}, u32[]{:S(2)}, u32[]{:S(2)}) async-start(bf16[32,32,128]{2,1,0:T(8,128)(2,1)} %select_convert_fusion), calls=%async_computation | async-start | bytes 524288 | tf_op jit(solution)/shard_map/all_to_all | solution.py:292
  16.5 12.6 %copy-start.3 = (f32[128]{0:T(128)S(1)}, f32[128]{0:T(128)}, u32[]{:S(2)}) copy-start(f32[128]{0:T(128)} %param.13) | copy-start | bytes 1540
  16.6 12.6 %copy-start.4 = (f32[128]{0:T(128)S(1)}, f32[128]{0:T(128)}, u32[]{:S(2)}) copy-start(f32[128]{0:T(128)} %param.15) | copy-start | bytes 1540
  18.7 39.3 %copy-start = (f32[4096]{0:T(1024)S(1)}, f32[4096]{0:T(1024)}, u32[]{:S(2)}) copy-start(f32[4096]{0:T(1024)} %param.17) | copy-start | bytes 49156
  18.7 39.3 %copy-start.1 = (f32[4096]{0:T(1024)S(1)}, f32[4096]{0:T(1024)}, u32[]{:S(2)}) copy-start(f32[4096]{0:T(1024)} %param.14) | copy-start | bytes 49156
  18.7 39.3 %copy-start.2 = (f32[4096]{0:T(1024)S(1)}, f32[4096]{0:T(1024)}, u32[]{:S(2)}) copy-start(f32[4096]{0:T(1024)} %param.16) | copy-start | bytes 49156

commit v6 on v5

--- a/solution.py
+++ b/solution.py
@@ -47,15 +47,19 @@
 
 
 AHEAD = 6
-LEAD = 20
-SITE_LEAD = 4
+SITE_ORDER = (4, 6, 0, 2, 5, 7, 1, 3)
+
+
+def peer(j):
+    chip = ((j >> 1) + 10) & 15
+    y, x = chip >> 2, chip & 3
+    return 8 * y + 2 * (x ^ (3 * (y & 1))) + (j & 1)
 
 
 def fetch(m_hbm, buf, sems, first, last):
     copies = []
-    pairs = m_hbm.shape[0] // 2
     for c, j in enumerate(range(first, last, 2)):
-        part = (m_hbm.at[pl.ds(2 * ((j + LEAD) % pairs), 4)], buf.at[pl.ds(2 * (j - first), 4)])
+        part = (m_hbm.at[pl.ds(2 * peer(j), 4)], buf.at[pl.ds(2 * (j - first), 4)])
         copies.append(pltpu.make_async_copy(*part, sems.at[c]))
     for copy in copies[:AHEAD]:
         copy.start()
@@ -107,10 +111,6 @@
     onehot = (ids_ref[...] == iota((patterns, 128), 0)).astype(BF16)
     half_gain[...] = 0.5 * gain_pick(gain_ref[...], onehot)
     wide = jnp.broadcast_to(pos_ref[...].astype(F32), (128, slots)).astype(BF16)
-
-    def peer(j):
-        return jnp.where(j + LEAD < slots // 2, j + LEAD, j + LEAD - slots // 2)
-
     slot, row = iota((4 * slots, slots), 1), iota((4 * slots, slots), 0)
     map_ref[...] = dot((slot == 2 * peer(row >> 3) + ((row >> 1) & 1)).astype(BF16), wide, ((1,), (1,)))
     slot, row = iota((2 * slots, slots), 1), iota((2 * slots, slots), 0)
@@ -284,15 +284,14 @@
 ):
     slots = margins.shape[0]
     rows = 4 * slots
-    pix_order = [[(j + LEAD) % n_pix for j in range(n_pix)]]
-    site_order = [[(j + SITE_LEAD) % n_site for j in range(n_site)]]
+    pix_order = [[peer(j) for j in range(n_pix)]]
 
     def to_pix(x):
         x = x.reshape(n_pix, -1, 128)
         return lax.all_to_all(x, "pix", 0, 0, tiled=True, axis_index_groups=pix_order).reshape(-1, 128)
 
     def to_site(x):
-        return lax.all_to_all(x, "site", 0, 0, tiled=True, axis_index_groups=site_order)
+        return lax.all_to_all(x, "site", 0, 0, tiled=True, axis_index_groups=[SITE_ORDER])
 
     price, site0 = site_price.reshape(1, 128), site_start.reshape(1, 128)
     dual0, weight, pixel0 = (v.reshape(32, 128) for v in (dual_start, weights, pixel_start))

time: 105 us -> 104 us (level)
  blocking collectives: 81.4 us -> 79.9 us
    all_to_all x2, blocking collectives: 27.4 us -> 25.3 us  [to_site(): lax.all_to_all(x, 'site', 0, 0, tiled=True, axis_index_groups=[SITE_ORDER])]
where the time goes in v6:
time: 104 us; the launch traced here: 103 us
  blocking collectives  79.9 us (77%)
  starting transfers between devices  10.4 us (10%)
  Pallas kernels  10.4 us (10%)
  other arithmetic  1.45 us (1%)
    all_to_all x5, blocking collectives, to_pix(): lax.all_to_all(x, 'pix', 0, 0, tiled=True, axis_index_groups=pix_order)  54.6 us
    all_to_all x2, blocking collectives, to_site(): lax.all_to_all(x, 'site', 0, 0, tiled=True, axis_index_groups=[SITE_ORDER])  25.3 us
    pallas_call x9, Pallas kernels, call(): pl.pallas_call(body, out_shape=[jax.ShapeDtypeStruct(*o) for o in outs],...  10.4 us
    all_to_all x1, starting transfers between devices, to_pix(): lax.all_to_all(x, 'pix', 0, 0, tiled=True, axis_index_groups=pix_order)  10.4 us
  transfers between devices with their start and end apart: 1, of which 1 were waited for; matrix products, arithmetic and copies ran while one was open for 0% of the time, Pallas kernels for 4%

profile of v6, /device:TPU:1, one launch (start us, length us, event | category | flops | bytes accessed | tf_op | source)
XLA Modules:
  0.0 103.0 jit_solution(5826523137688858937)
XLA Ops:
  0.6 1.4 %select_convert_fusion = bf16[32,32,128]{2,1,0:T(8,128)(2,1)} fusion(f32[32,128]{1,0:T(8,128)} %bitcast.30), kind=kLoop, calls=%fused_computation | loop fusion | flops 524288 | bytes 278528 | tf_op jit(solution)/shard_map/convert_element_type | solution.py:302
  2.1 10.4 %all-to-all-start = ((bf16[32,32,128]{2,1,0:T(8,128)(2,1)}), bf16[32,32,128]{2,1,0:T(8,128)(2,1)S(1)}, u32[]{:S(2)}, u32[]{:S(2)}) async-start(bf16[32,32,128]{2,1,0:T(8,128)(2,1)} %select_convert_fusion), calls=%async_computation | async-start | bytes 524288 | tf_op jit(solution)/shard_map/all_to_all | solution.py:291
  12.4 3.9 %shard_map.112 = (bf16[22,256,256]{2,1,0:T(8,128)(2,1)S(1)}, f32[256,128]{1,0:T(8,128)S(1)}, f32[128,128]{1,0:T(8,128)S(1)}, f32[256,128]{1,0:T(8,128)S(1)}) custom-call(s32[64,256,128]{2,1,0:T(8,128)} %m_hbm.3, s32[1,64]{1,0:T(1,128)} %bitcast.41, s32[1,128]{1,0:T(1,128)} %bitcast.42, f32[16,256]{1,0:T(8,128)} %gain_hbm.1), custom_call_target="tpu_custom_call" | custom-call | flops 20971520 | bytes 12582912 | tf_op jit(solution)/shard_map/pallas_call | solution.py:34
  16.3 0.1 all-to-all-done.ag_ref
  16.5 0.0 copy-start.3
  16.5 0.0 copy-start.4
  16.5 2.1 %shard_map.113 = (f32[128,128]{1,0:T(8,128)S(1)}, bf16[10,256,256]{2,1,0:T(8,128)(2,1)S(1)}) custom-call(bf16[32,32,128]{2,1,0:T(8,128)(2,1)S(1)} %all-to-all-done.ag_ref, f32[256,128]{1,0:T(8,128)S(1)} %get-tuple-element.22.map_ref, f32[128,128]{1,0:T(8,128)S(1)} %get-tuple-element.23.note_ref, f32[256,128]{1,0:T(8,128)S(1)} %get-tuple-element.24.half_gain, ...), custom_call_target="tpu_custom_call" | custom-call | tf_op jit(solution)/shard_map/pallas_call | solution.py:34
  18.6 0.0 copy-start
  18.6 0.0 copy-start.1
  18.6 0.0 copy-start.2
  18.6 10.6 %all_to_all.40 = f32[32,4,128]{2,1,0:T(4,128)S(1)} all-to-all(f32[32,4,128]{2,1,0:T(4,128)S(1)} %bitcast.35), channel_id=1, replica_groups={{160,168,176,184,240,248,224,232,208,216,192,200,0,8,16,24,32,40,48,56,..., dimensions={0} | all-to-all | bytes 131072 | tf_op jit(solution)/shard_map/all_to_all | solution.py:291
  29.2 0.0 copy-done.3
  29.2 0.0 copy-done.4
  29.2 1.2 %shard_map.114 = (f32[256,128]{1,0:T(8,128)S(1)}, f32[1,128]{1,0:T(1,128)S(1)}, f32[1,128]{1,0:T(1,128)S(1)}) custom-call(f32[128,128]{1,0:T(8,128)S(1)} %bitcast.22, f32[1,128]{1,0:T(1,128)S(1)} %bitcast.38, f32[1,128]{1,0:T(1,128)S(1)} %bitcast.40, bf16[22,256,256]{2,1,0:T(8,128)(2,1)S(1)} %get-tuple-element.25.near_ref, ...), custom_call_target="tpu_custom_call" | custom-call | tf_op jit(solution)/shard_map/pallas_call | solution.py:34
  30.4 11.1 %all_to_all.41 = f32[32,8,128]{2,1,0:T(8,128)S(1)} all-to-all(f32[32,8,128]{2,1,0:T(8,128)S(1)} %bitcast.27), channel_id=1, replica_groups={{160,168,176,184,240,248,224,232,208,216,192,200,0,8,16,24,32,40,48,56,..., dimensions={0} | all-to-all | bytes 262144 | tf_op jit(solution)/shard_map/all_to_all | solution.py:291
  41.5 0.4 shard_map.115
  41.9 15.5 %all_to_all.42.in_ref = f32[8,64,128]{2,1,0:T(8,128)S(1)} all-to-all(f32[8,64,128]{2,1,0:T(8,128)S(1)} %get-tuple-element.29), channel_id=1, replica_groups={{4,6,0,2,5,7,1,3},{12,14,8,10,13,15,9,11},{20,22,16,18,21,23,17,19},{28..., dimensions={0} | all-to-all | bytes 524288 | tf_op jit(solution)/shard_map/all_to_all | solution.py:294
  57.3 0.0 copy-done
  57.3 0.0 copy-done.1
  57.3 0.0 copy-done.2
  57.3 0.1 shard_map.116
  57.5 11.8 %all_to_all.43 = f32[32,4,128]{2,1,0:T(4,128)S(1)} all-to-all(f32[32,4,128]{2,1,0:T(4,128)S(1)} %bitcast.36), channel_id=1, replica_groups={{160,168,176,184,240,248,224,232,208,216,192,200,0,8,16,24,32,40,48,56,..., dimensions={0} | all-to-all | bytes 131072 | tf_op jit(solution)/shard_map/all_to_all | solution.py:291
  69.3 0.7 shard_map.117
  70.0 10.2 %all_to_all.44 = f32[32,1,128]{2,1,0:T(1,128)S(1)} all-to-all(f32[32,1,128]{2,1,0:T(1,128)S(1)} %bitcast.29), channel_id=1, replica_groups={{160,168,176,184,240,248,224,232,208,216,192,200,0,8,16,24,32,40,48,56,..., dimensions={0} | all-to-all | bytes 32768 | tf_op jit(solution)/shard_map/all_to_all | solution.py:291
  80.2 1.2 %shard_map.118 = (f32[128,128]{1,0:T(8,128)S(1)}, f32[1,128]{1,0:T(1,128)}) custom-call(f32[32,128]{1,0:T(8,128)S(1)} %bitcast.28, f32[1,128]{1,0:T(1,128)S(1)} %bitcast.39, f32[1,128]{1,0:T(1,128)S(1)} %get-tuple-element.32.site_ref, f32[1,128]{1,0:T(1,128)S(1)} %get-tuple-element.33.sum_ref, bf16[22,256,256]{2,1,0:T(8,128)(2,1)S(1)} %get-tuple-element.25.near_ref, ...), custom_call_target="tpu_custom_call" | custom-call | tf_op jit(solution)/shard_map/pallas_call | solution.py:34
  81.3 11.0 %all_to_all.45 = f32[32,4,128]{2,1,0:T(4,128)S(1)} all-to-all(f32[32,4,128]{2,1,0:T(4,128)S(1)} %bitcast.34), channel_id=1, replica_groups={{160,168,176,184,240,248,224,232,208,216,192,200,0,8,16,24,32,40,48,56,..., dimensions={0} | all-to-all | bytes 131072 | tf_op jit(solution)/shard_map/all_to_all | solution.py:291
  92.3 0.2 shard_map.119
  92.5 9.8 %all_to_all.46.in_ref = f32[8,32,128]{2,1,0:T(8,128)S(1)} all-to-all(f32[8,32,128]{2,1,0:T(8,128)S(1)} %shard_map.119), channel_id=1, replica_groups={{4,6,0,2,5,7,1,3},{12,14,8,10,13,15,9,11},{20,22,16,18,21,23,17,19},{28..., dimensions={0} | all-to-all | bytes 262144 | tf_op jit(solution)/shard_map/all_to_all | solution.py:294
  102.4 0.6 shard_map.120
Async XLA Ops:
  2.1 14.4 %all-to-all-start = ((bf16[32,32,128]{2,1,0:T(8,128)(2,1)}), bf16[32,32,128]{2,1,0:T(8,128)(2,1)S(1)}, u32[]{:S(2)}, u32[]{:S(2)}) async-start(bf16[32,32,128]{2,1,0:T(8,128)(2,1)} %select_convert_fusion), calls=%async_computation | async-start | bytes 524288 | tf_op jit(solution)/shard_map/all_to_all | solution.py:291
  16.5 12.8 %copy-start.3 = (f32[128]{0:T(128)S(1)}, f32[128]{0:T(128)}, u32[]{:S(2)}) copy-start(f32[128]{0:T(128)} %param.13) | copy-start | bytes 1540
  16.5 12.8 %copy-start.4 = (f32[128]{0:T(128)S(1)}, f32[128]{0:T(128)}, u32[]{:S(2)}) copy-start(f32[128]{0:T(128)} %param.15) | copy-start | bytes 1540
  18.6 38.7 %copy-start = (f32[4096]{0:T(1024)S(1)}, f32[4096]{0:T(1024)}, u32[]{:S(2)}) copy-start(f32[4096]{0:T(1024)} %param.17) | copy-start | bytes 49156
  18.6 38.7 %copy-start.1 = (f32[4096]{0:T(1024)S(1)}, f32[4096]{0:T(1024)}, u32[]{:S(2)}) copy-start(f32[4096]{0:T(1024)} %param.14) | copy-start | bytes 49156
  18.6 38.7 %copy-start.2 = (f32[4096]{0:T(1024)S(1)}, f32[4096]{0:T(1024)}, u32[]{:S(2)}) copy-start(f32[4096]{0:T(1024)} %param.16) | copy-start | bytes 49156

commit v7 on v6

--- a/solution.py
+++ b/solution.py
@@ -47,7 +47,7 @@
 
 
 AHEAD = 6
-SITE_ORDER = (4, 6, 0, 2, 5, 7, 1, 3)
+SITE_ORDER = (4, 0, 2, 7, 1, 6, 3, 5)
 
 
 def peer(j):
@@ -76,7 +76,7 @@
     def pair(n, carry):
         gain = half_gain[...]
         level = jnp.concatenate([buf[2 * n + i].astype(F32) * HALF_SCALE + gain for i in range(2)], axis=1)
-        out_ref[n] = (0.5 * jnp.tanh(level) + 0.5).astype(BF16)
+        out_ref[n] = (jnp.tanh(level) + 1.0).astype(BF16)
         return carry
 
     pair(t, 0)
@@ -150,9 +150,9 @@
 
 def push(row, plain, cov, out_ref):
     spot = iota((8, 128), 0)
-    value = jnp.broadcast_to(row, (8, 128))
+    value = jnp.broadcast_to(0.5 * row, (8, 128))
     if plain:
-        value = jnp.where(spot < 4, 1.0, value)
+        value = jnp.where(spot < 4, 0.5, value)
     own = (spot & 2) == 0
     left = jnp.concatenate([jnp.where(own, value, 0.0), jnp.where(own, 0.0, value)], axis=1).astype(BF16)
     first = (spot & 1) == 0
@@ -240,12 +240,13 @@
     new_pixel, new_dual = step(pixel_ref[...], dual_ref[...], weight_ref[...], totals[32:], row_sum)
     new_pixel_ref[...] = new_pixel
     new_dual_ref[...] = new_dual
-    out_ref[...] = dot(chooser(key_ref), new_dual.astype(BF16))
-
-
-def pull_kernel(x_ref, near_ref, far_ref, out_ref):
+    out_ref[...] = dot(chooser(key_ref), new_dual.astype(BF16)).astype(BF16)
+
+
+def pull_kernel(x_ref, near_ref, far_ref, out_ref, rows_ref):
     cov = tiles(near_ref, far_ref)
-    total = pull([x_ref[t * 4 : (t + 1) * 4, :] for t in range(len(cov))], cov)
+    rows_ref[...] = x_ref[...].astype(F32)
+    total = pull([rows_ref[t * 4 : (t + 1) * 4, :] for t in range(len(cov))], cov)
     out_ref[...] = jnp.broadcast_to(own_columns(total, 0), out_ref.shape)
 
 
@@ -340,9 +341,9 @@
     out, site1, column_sum = call(first_push_kernel, [message, line, line], summed, price, site0, *cov)
     out, key = call(first_spread_kernel, [((n_site, 64, 128), F32), half_message], to_pix(out), summed)
     out, dual1, pixel1, row_sum = call(
-        first_dual_kernel, [half_message] + [vector] * 3, to_site(out), key, dual0, weight, pixel0
-    )
-    (out,) = call(pull_kernel, [((n_pix, 128), F32)], to_pix(out), *cov)
+        first_dual_kernel, [((2 * slots, 128), BF16)] + [vector] * 3, to_site(out), key, dual0, weight, pixel0
+    )
+    (out,) = call(pull_kernel, [((n_pix, 128), F32)], to_pix(out), *cov, scratch=[pltpu.VMEM((2 * slots, 128), F32)])
     out, site2 = call(push_kernel, [half_message, line], to_pix(out), price, site1, column_sum, *cov)
     (out,) = call(spread_kernel, [((n_site, 32, 128), F32)], to_pix(out), key)
     dual2, pixel2 = call(dual_kernel, [vector] * 2, to_site(out), row_sum, dual1, weight, pixel1)

time: 104 us -> 104 us (level)
  no operation moved by 1% of the time
where the time goes in v7:
time: 104 us; the launch traced here: 103 us
  blocking collectives  80.2 us (77%)
  starting transfers between devices  10.4 us (10%)
  Pallas kernels  10.4 us (10%)
  other arithmetic  1.45 us (1%)
    all_to_all x5, blocking collectives, to_pix(): lax.all_to_all(x, 'pix', 0, 0, tiled=True, axis_index_groups=pix_order)  55.2 us
    all_to_all x2, blocking collectives, to_site(): lax.all_to_all(x, 'site', 0, 0, tiled=True, axis_index_groups=[SITE_ORDER])  25 us
    pallas_call x9, Pallas kernels, call(): pl.pallas_call(body, out_shape=[jax.ShapeDtypeStruct(*o) for o in outs],...  10.4 us
    all_to_all x1, starting transfers between devices, to_pix(): lax.all_to_all(x, 'pix', 0, 0, tiled=True, axis_index_groups=pix_order)  10.4 us
  transfers between devices with their start and end apart: 1, of which 1 were waited for; matrix products, arithmetic and copies ran while one was open for 0% of the time, Pallas kernels for 4%

profile of v7, /device:TPU:1, one launch (start us, length us, event | category | flops | bytes accessed | tf_op | source)
XLA Modules:
  0.0 103.2 jit_solution(17713878019250253916)
XLA Ops:
  0.6 1.4 %select_convert_fusion = bf16[32,32,128]{2,1,0:T(8,128)(2,1)} fusion(f32[32,128]{1,0:T(8,128)} %bitcast.30), kind=kLoop, calls=%fused_computation | loop fusion | flops 524288 | bytes 278528 | tf_op jit(solution)/shard_map/convert_element_type | solution.py:303
  2.1 10.4 %all-to-all-start = ((bf16[32,32,128]{2,1,0:T(8,128)(2,1)}), bf16[32,32,128]{2,1,0:T(8,128)(2,1)S(1)}, u32[]{:S(2)}, u32[]{:S(2)}) async-start(bf16[32,32,128]{2,1,0:T(8,128)(2,1)} %select_convert_fusion), calls=%async_computation | async-start | bytes 524288 | tf_op jit(solution)/shard_map/all_to_all | solution.py:292
  12.4 3.8 %shard_map.112 = (bf16[22,256,256]{2,1,0:T(8,128)(2,1)S(1)}, f32[256,128]{1,0:T(8,128)S(1)}, f32[128,128]{1,0:T(8,128)S(1)}, f32[256,128]{1,0:T(8,128)S(1)}) custom-call(s32[64,256,128]{2,1,0:T(8,128)} %m_hbm.3, s32[1,64]{1,0:T(1,128)} %bitcast.41, s32[1,128]{1,0:T(1,128)} %bitcast.42, f32[16,256]{1,0:T(8,128)} %gain_hbm.1), custom_call_target="tpu_custom_call" | custom-call | flops 20971520 | bytes 12582912 | tf_op jit(solution)/shard_map/pallas_call | solution.py:34
  16.3 0.2 all-to-all-done.ag_ref
  16.5 0.0 copy-start.3
  16.5 0.0 copy-start.4
  16.5 2.1 %shard_map.113 = (f32[128,128]{1,0:T(8,128)S(1)}, bf16[10,256,256]{2,1,0:T(8,128)(2,1)S(1)}) custom-call(bf16[32,32,128]{2,1,0:T(8,128)(2,1)S(1)} %all-to-all-done.ag_ref, f32[256,128]{1,0:T(8,128)S(1)} %get-tuple-element.22.map_ref, f32[128,128]{1,0:T(8,128)S(1)} %get-tuple-element.23.note_ref, f32[256,128]{1,0:T(8,128)S(1)} %get-tuple-element.24.half_gain, ...), custom_call_target="tpu_custom_call" | custom-call | tf_op jit(solution)/shard_map/pallas_call | solution.py:34
  18.6 0.0 copy-start
  18.6 0.0 copy-start.1
  18.6 0.0 copy-start.2
  18.6 10.6 %all_to_all.40 = f32[32,4,128]{2,1,0:T(4,128)S(1)} all-to-all(f32[32,4,128]{2,1,0:T(4,128)S(1)} %bitcast.35), channel_id=1, replica_groups={{160,168,176,184,240,248,224,232,208,216,192,200,0,8,16,24,32,40,48,56,..., dimensions={0} | all-to-all | bytes 131072 | tf_op jit(solution)/shard_map/all_to_all | solution.py:292
  29.2 0.0 copy-done.3
  29.2 0.0 copy-done.4
  29.2 1.2 %shard_map.114 = (f32[256,128]{1,0:T(8,128)S(1)}, f32[1,128]{1,0:T(1,128)S(1)}, f32[1,128]{1,0:T(1,128)S(1)}) custom-call(f32[128,128]{1,0:T(8,128)S(1)} %bitcast.22, f32[1,128]{1,0:T(1,128)S(1)} %bitcast.38, f32[1,128]{1,0:T(1,128)S(1)} %bitcast.40, bf16[22,256,256]{2,1,0:T(8,128)(2,1)S(1)} %get-tuple-element.25.near_ref, ...), custom_call_target="tpu_custom_call" | custom-call | tf_op jit(solution)/shard_map/pallas_call | solution.py:34
  30.4 11.1 %all_to_all.41 = f32[32,8,128]{2,1,0:T(8,128)S(1)} all-to-all(f32[32,8,128]{2,1,0:T(8,128)S(1)} %bitcast.27), channel_id=1, replica_groups={{160,168,176,184,240,248,224,232,208,216,192,200,0,8,16,24,32,40,48,56,..., dimensions={0} | all-to-all | bytes 262144 | tf_op jit(solution)/shard_map/all_to_all | solution.py:292
  41.5 0.4 shard_map.115
  41.9 14.9 %all_to_all.42.in_ref = f32[8,64,128]{2,1,0:T(8,128)S(1)} all-to-all(f32[8,64,128]{2,1,0:T(8,128)S(1)} %get-tuple-element.29), channel_id=1, replica_groups={{4,0,2,7,1,6,3,5},{12,8,10,15,9,14,11,13},{20,16,18,23,17,22,19,21},{28..., dimensions={0} | all-to-all | bytes 524288 | tf_op jit(solution)/shard_map/all_to_all | solution.py:295
  56.8 0.0 copy-done
  56.8 0.0 copy-done.1
  56.8 0.0 copy-done.2
  56.8 0.1 shard_map.116
  57.0 12.3 %all_to_all.43 = bf16[32,4,128]{2,1,0:T(4,128)(2,1)S(1)} all-to-all(bf16[32,4,128]{2,1,0:T(4,128)(2,1)S(1)} %bitcast.36), channel_id=1, replica_groups={{160,168,176,184,240,248,224,232,208,216,192,200,0,8,16,24,32,40,48,56,..., dimensions={0} | all-to-all | bytes 65536 | tf_op jit(solution)/shard_map/all_to_all | solution.py:292
  69.2 0.7 shard_map.117
  69.9 10.2 %all_to_all.44 = f32[32,1,128]{2,1,0:T(1,128)S(1)} all-to-all(f32[32,1,128]{2,1,0:T(1,128)S(1)} %bitcast.29), channel_id=1, replica_groups={{160,168,176,184,240,248,224,232,208,216,192,200,0,8,16,24,32,40,48,56,..., dimensions={0} | all-to-all | bytes 32768 | tf_op jit(solution)/shard_map/all_to_all | solution.py:292
  80.1 1.2 %shard_map.118 = (f32[128,128]{1,0:T(8,128)S(1)}, f32[1,128]{1,0:T(1,128)}) custom-call(f32[32,128]{1,0:T(8,128)S(1)} %bitcast.28, f32[1,128]{1,0:T(1,128)S(1)} %bitcast.39, f32[1,128]{1,0:T(1,128)S(1)} %get-tuple-element.32.site_ref, f32[1,128]{1,0:T(1,128)S(1)} %get-tuple-element.33.sum_ref, bf16[22,256,256]{2,1,0:T(8,128)(2,1)S(1)} %get-tuple-element.25.near_ref, ...), custom_call_target="tpu_custom_call" | custom-call | tf_op jit(solution)/shard_map/pallas_call | solution.py:34
  81.3 11.0 %all_to_all.45 = f32[32,4,128]{2,1,0:T(4,128)S(1)} all-to-all(f32[32,4,128]{2,1,0:T(4,128)S(1)} %bitcast.34), channel_id=1, replica_groups={{160,168,176,184,240,248,224,232,208,216,192,200,0,8,16,24,32,40,48,56,..., dimensions={0} | all-to-all | bytes 131072 | tf_op jit(solution)/shard_map/all_to_all | solution.py:292
  92.3 0.2 shard_map.119
  92.5 10.1 %all_to_all.46.in_ref = f32[8,32,128]{2,1,0:T(8,128)S(1)} all-to-all(f32[8,32,128]{2,1,0:T(8,128)S(1)} %shard_map.119), channel_id=1, replica_groups={{4,0,2,7,1,6,3,5},{12,8,10,15,9,14,11,13},{20,16,18,23,17,22,19,21},{28..., dimensions={0} | all-to-all | bytes 262144 | tf_op jit(solution)/shard_map/all_to_all | solution.py:295
  102.6 0.6 shard_map.120
Async XLA Ops:
  2.1 14.4 %all-to-all-start = ((bf16[32,32,128]{2,1,0:T(8,128)(2,1)}), bf16[32,32,128]{2,1,0:T(8,128)(2,1)S(1)}, u32[]{:S(2)}, u32[]{:S(2)}) async-start(bf16[32,32,128]{2,1,0:T(8,128)(2,1)} %select_convert_fusion), calls=%async_computation | async-start | bytes 524288 | tf_op jit(solution)/shard_map/all_to_all | solution.py:292
  16.5 12.8 %copy-start.3 = (f32[128]{0:T(128)S(1)}, f32[128]{0:T(128)}, u32[]{:S(2)}) copy-start(f32[128]{0:T(128)} %param.13) | copy-start | bytes 1540
  16.5 12.8 %copy-start.4 = (f32[128]{0:T(128)S(1)}, f32[128]{0:T(128)}, u32[]{:S(2)}) copy-start(f32[128]{0:T(128)} %param.15) | copy-start | bytes 1540
  18.6 38.2 %copy-start = (f32[4096]{0:T(1024)S(1)}, f32[4096]{0:T(1024)}, u32[]{:S(2)}) copy-start(f32[4096]{0:T(1024)} %param.17) | copy-start | bytes 49156
  18.6 38.2 %copy-start.1 = (f32[4096]{0:T(1024)S(1)}, f32[4096]{0:T(1024)}, u32[]{:S(2)}) copy-start(f32[4096]{0:T(1024)} %param.14) | copy-start | bytes 49156
  18.6 38.2 %copy-start.2 = (f32[4096]{0:T(1024)S(1)}, f32[4096]{0:T(1024)}, u32[]{:S(2)}) copy-start(f32[4096]{0:T(1024)} %param.16) | copy-start | bytes 49156

commit v8 on v7

--- a/solution.py
+++ b/solution.py
@@ -47,7 +47,7 @@
 
 
 AHEAD = 6
-SITE_ORDER = (4, 0, 2, 7, 1, 6, 3, 5)
+SITE_ORDER = (6, 4, 0, 2, 5, 7, 1, 3)
 
 
 def peer(j):

time: 104 us -> 104 us (level)
  no operation moved by 1% of the time
where the time goes in v8:
time: 104 us; the launch traced here: 102 us
  blocking collectives  79.4 us (76%)
  starting transfers between devices  10.4 us (10%)
  Pallas kernels  10.4 us (10%)
  other arithmetic  1.45 us (1%)
    all_to_all x5, blocking collectives, to_pix(): lax.all_to_all(x, 'pix', 0, 0, tiled=True, axis_index_groups=pix_order)  54.8 us
    all_to_all x2, blocking collectives, to_site(): lax.all_to_all(x, 'site', 0, 0, tiled=True, axis_index_groups=[SITE_ORDER])  24.6 us
    pallas_call x9, Pallas kernels, call(): pl.pallas_call(body, out_shape=[jax.ShapeDtypeStruct(*o) for o in outs],...  10.4 us
    all_to_all x1, starting transfers between devices, to_pix(): lax.all_to_all(x, 'pix', 0, 0, tiled=True, axis_index_groups=pix_order)  10.4 us
  transfers between devices with their start and end apart: 1, of which 1 were waited for; matrix products, arithmetic and copies ran while one was open for 0% of the time, Pallas kernels for 4%

profile of v8, /device:TPU:1, one launch (start us, length us, event | category | flops | bytes accessed | tf_op | source)
XLA Modules:
  0.0 102.5 jit_solution(17367959723435674208)
XLA Ops:
  0.6 1.4 %select_convert_fusion = bf16[32,32,128]{2,1,0:T(8,128)(2,1)} fusion(f32[32,128]{1,0:T(8,128)} %bitcast.30), kind=kLoop, calls=%fused_computation | loop fusion | flops 524288 | bytes 278528 | tf_op jit(solution)/shard_map/convert_element_type | solution.py:303
  2.1 10.4 %all-to-all-start = ((bf16[32,32,128]{2,1,0:T(8,128)(2,1)}), bf16[32,32,128]{2,1,0:T(8,128)(2,1)S(1)}, u32[]{:S(2)}, u32[]{:S(2)}) async-start(bf16[32,32,128]{2,1,0:T(8,128)(2,1)} %select_convert_fusion), calls=%async_computation | async-start | bytes 524288 | tf_op jit(solution)/shard_map/all_to_all | solution.py:292
  12.4 3.8 %shard_map.112 = (bf16[22,256,256]{2,1,0:T(8,128)(2,1)S(1)}, f32[256,128]{1,0:T(8,128)S(1)}, f32[128,128]{1,0:T(8,128)S(1)}, f32[256,128]{1,0:T(8,128)S(1)}) custom-call(s32[64,256,128]{2,1,0:T(8,128)} %m_hbm.3, s32[1,64]{1,0:T(1,128)} %bitcast.41, s32[1,128]{1,0:T(1,128)} %bitcast.42, f32[16,256]{1,0:T(8,128)} %gain_hbm.1), custom_call_target="tpu_custom_call" | custom-call | flops 20971520 | bytes 12582912 | tf_op jit(solution)/shard_map/pallas_call | solution.py:34
  16.3 0.2 all-to-all-done.ag_ref
  16.5 0.0 copy-start.3
  16.5 0.0 copy-start.4
  16.5 2.1 %shard_map.113 = (f32[128,128]{1,0:T(8,128)S(1)}, bf16[10,256,256]{2,1,0:T(8,128)(2,1)S(1)}) custom-call(bf16[32,32,128]{2,1,0:T(8,128)(2,1)S(1)} %all-to-all-done.ag_ref, f32[256,128]{1,0:T(8,128)S(1)} %get-tuple-element.22.map_ref, f32[128,128]{1,0:T(8,128)S(1)} %get-tuple-element.23.note_ref, f32[256,128]{1,0:T(8,128)S(1)} %get-tuple-element.24.half_gain, ...), custom_call_target="tpu_custom_call" | custom-call | tf_op jit(solution)/shard_map/pallas_call | solution.py:34
  18.6 0.0 copy-start
  18.6 0.0 copy-start.1
  18.6 0.0 copy-start.2
  18.6 10.6 %all_to_all.40 = f32[32,4,128]{2,1,0:T(4,128)S(1)} all-to-all(f32[32,4,128]{2,1,0:T(4,128)S(1)} %bitcast.35), channel_id=1, replica_groups={{160,168,176,184,240,248,224,232,208,216,192,200,0,8,16,24,32,40,48,56,..., dimensions={0} | all-to-all | bytes 131072 | tf_op jit(solution)/shard_map/all_to_all | solution.py:292
  29.2 0.0 copy-done.3
  29.2 0.0 copy-done.4
  29.2 1.2 %shard_map.114 = (f32[256,128]{1,0:T(8,128)S(1)}, f32[1,128]{1,0:T(1,128)S(1)}, f32[1,128]{1,0:T(1,128)S(1)}) custom-call(f32[128,128]{1,0:T(8,128)S(1)} %bitcast.22, f32[1,128]{1,0:T(1,128)S(1)} %bitcast.38, f32[1,128]{1,0:T(1,128)S(1)} %bitcast.40, bf16[22,256,256]{2,1,0:T(8,128)(2,1)S(1)} %get-tuple-element.25.near_ref, ...), custom_call_target="tpu_custom_call" | custom-call | tf_op jit(solution)/shard_map/pallas_call | solution.py:34
  30.4 11.1 %all_to_all.41 = f32[32,8,128]{2,1,0:T(8,128)S(1)} all-to-all(f32[32,8,128]{2,1,0:T(8,128)S(1)} %bitcast.27), channel_id=1, replica_groups={{160,168,176,184,240,248,224,232,208,216,192,200,0,8,16,24,32,40,48,56,..., dimensions={0} | all-to-all | bytes 262144 | tf_op jit(solution)/shard_map/all_to_all | solution.py:292
  41.5 0.4 shard_map.115
  41.9 14.5 %all_to_all.42.in_ref = f32[8,64,128]{2,1,0:T(8,128)S(1)} all-to-all(f32[8,64,128]{2,1,0:T(8,128)S(1)} %get-tuple-element.29), channel_id=1, replica_groups={{6,4,0,2,5,7,1,3},{14,12,8,10,13,15,9,11},{22,20,16,18,21,23,17,19},{30..., dimensions={0} | all-to-all | bytes 524288 | tf_op jit(solution)/shard_map/all_to_all | solution.py:295
  56.3 0.0 copy-done
  56.3 0.0 copy-done.1
  56.3 0.0 copy-done.2
  56.3 0.1 shard_map.116
  56.5 11.9 %all_to_all.43 = bf16[32,4,128]{2,1,0:T(4,128)(2,1)S(1)} all-to-all(bf16[32,4,128]{2,1,0:T(4,128)(2,1)S(1)} %bitcast.36), channel_id=1, replica_groups={{160,168,176,184,240,248,224,232,208,216,192,200,0,8,16,24,32,40,48,56,..., dimensions={0} | all-to-all | bytes 65536 | tf_op jit(solution)/shard_map/all_to_all | solution.py:292
  68.4 0.7 shard_map.117
  69.1 10.2 %all_to_all.44 = f32[32,1,128]{2,1,0:T(1,128)S(1)} all-to-all(f32[32,1,128]{2,1,0:T(1,128)S(1)} %bitcast.29), channel_id=1, replica_groups={{160,168,176,184,240,248,224,232,208,216,192,200,0,8,16,24,32,40,48,56,..., dimensions={0} | all-to-all | bytes 32768 | tf_op jit(solution)/shard_map/all_to_all | solution.py:292
  79.3 1.2 %shard_map.118 = (f32[128,128]{1,0:T(8,128)S(1)}, f32[1,128]{1,0:T(1,128)}) custom-call(f32[32,128]{1,0:T(8,128)S(1)} %bitcast.28, f32[1,128]{1,0:T(1,128)S(1)} %bitcast.39, f32[1,128]{1,0:T(1,128)S(1)} %get-tuple-element.32.site_ref, f32[1,128]{1,0:T(1,128)S(1)} %get-tuple-element.33.sum_ref, bf16[22,256,256]{2,1,0:T(8,128)(2,1)S(1)} %get-tuple-element.25.near_ref, ...), custom_call_target="tpu_custom_call" | custom-call | tf_op jit(solution)/shard_map/pallas_call | solution.py:34
  80.5 11.0 %all_to_all.45 = f32[32,4,128]{2,1,0:T(4,128)S(1)} all-to-all(f32[32,4,128]{2,1,0:T(4,128)S(1)} %bitcast.34), channel_id=1, replica_groups={{160,168,176,184,240,248,224,232,208,216,192,200,0,8,16,24,32,40,48,56,..., dimensions={0} | all-to-all | bytes 131072 | tf_op jit(solution)/shard_map/all_to_all | solution.py:292
  91.5 0.2 shard_map.119
  91.7 10.2 %all_to_all.46.in_ref = f32[8,32,128]{2,1,0:T(8,128)S(1)} all-to-all(f32[8,32,128]{2,1,0:T(8,128)S(1)} %shard_map.119), channel_id=1, replica_groups={{6,4,0,2,5,7,1,3},{14,12,8,10,13,15,9,11},{22,20,16,18,21,23,17,19},{30..., dimensions={0} | all-to-all | bytes 262144 | tf_op jit(solution)/shard_map/all_to_all | solution.py:295
  101.9 0.6 shard_map.120
Async XLA Ops:
  2.1 14.4 %all-to-all-start = ((bf16[32,32,128]{2,1,0:T(8,128)(2,1)}), bf16[32,32,128]{2,1,0:T(8,128)(2,1)S(1)}, u32[]{:S(2)}, u32[]{:S(2)}) async-start(bf16[32,32,128]{2,1,0:T(8,128)(2,1)} %select_convert_fusion), calls=%async_computation | async-start | bytes 524288 | tf_op jit(solution)/shard_map/all_to_all | solution.py:292
  16.5 12.8 %copy-start.3 = (f32[128]{0:T(128)S(1)}, f32[128]{0:T(128)}, u32[]{:S(2)}) copy-start(f32[128]{0:T(128)} %param.13) | copy-start | bytes 1540
  16.5 12.8 %copy-start.4 = (f32[128]{0:T(128)S(1)}, f32[128]{0:T(128)}, u32[]{:S(2)}) copy-start(f32[128]{0:T(128)} %param.15) | copy-start | bytes 1540
  18.6 37.7 %copy-start = (f32[4096]{0:T(1024)S(1)}, f32[4096]{0:T(1024)}, u32[]{:S(2)}) copy-start(f32[4096]{0:T(1024)} %param.17) | copy-start | bytes 49156
  18.6 37.7 %copy-start.1 = (f32[4096]{0:T(1024)S(1)}, f32[4096]{0:T(1024)}, u32[]{:S(2)}) copy-start(f32[4096]{0:T(1024)} %param.14) | copy-start | bytes 49156
  18.6 37.7 %copy-start.2 = (f32[4096]{0:T(1024)S(1)}, f32[4096]{0:T(1024)}, u32[]{:S(2)}) copy-start(f32[4096]{0:T(1024)} %param.16) | copy-start | bytes 49156

commit v9 on v8

--- a/solution.py
+++ b/solution.py
@@ -53,13 +53,13 @@
 def peer(j):
     chip = ((j >> 1) + 10) & 15
     y, x = chip >> 2, chip & 3
-    return 8 * y + 2 * (x ^ (3 * (y & 1))) + (j & 1)
+    return 8 * y + 2 * (x ^ (3 * (y & 1))) + ((j & 1) ^ 1)
 
 
 def fetch(m_hbm, buf, sems, first, last):
     copies = []
     for c, j in enumerate(range(first, last, 2)):
-        part = (m_hbm.at[pl.ds(2 * peer(j), 4)], buf.at[pl.ds(2 * (j - first), 4)])
+        part = (m_hbm.at[pl.ds(2 * peer(j + 1), 4)], buf.at[pl.ds(2 * (j - first), 4)])
         copies.append(pltpu.make_async_copy(*part, sems.at[c]))
     for copy in copies[:AHEAD]:
         copy.start()
@@ -75,7 +75,7 @@
 def build(buf, out_ref, half_gain, t):
     def pair(n, carry):
         gain = half_gain[...]
-        level = jnp.concatenate([buf[2 * n + i].astype(F32) * HALF_SCALE + gain for i in range(2)], axis=1)
+        level = jnp.concatenate([buf[2 * (n ^ 1) + i].astype(F32) * HALF_SCALE + gain for i in range(2)], axis=1)
         out_ref[n] = (jnp.tanh(level) + 1.0).astype(BF16)
         return carry
 

time: 104 us -> 102 us (0.981)
  blocking collectives: 79.4 us -> 77.9 us
    all_to_all x5, blocking collectives: 54.8 us -> 53.4 us  [to_pix(): lax.all_to_all(x, 'pix', 0, 0, tiled=True, axis_index_groups=pix_order)]
where the time goes in v9:
time: 102 us; the launch traced here: 101 us
  blocking collectives  77.9 us (76%)
  Pallas kernels  10.4 us (10%)
  starting transfers between devices  9.89 us (10%)
  other arithmetic  1.45 us (1%)
    all_to_all x5, blocking collectives, to_pix(): lax.all_to_all(x, 'pix', 0, 0, tiled=True, axis_index_groups=pix_order)  53.4 us
    all_to_all x2, blocking collectives, to_site(): lax.all_to_all(x, 'site', 0, 0, tiled=True, axis_index_groups=[SITE_ORDER])  24.6 us
    pallas_call x9, Pallas kernels, call(): pl.pallas_call(body, out_shape=[jax.ShapeDtypeStruct(*o) for o in outs],...  10.4 us
    all_to_all x1, starting transfers between devices, to_pix(): lax.all_to_all(x, 'pix', 0, 0, tiled=True, axis_index_groups=pix_order)  9.89 us
  transfers between devices with their start and end apart: 1, of which 1 were waited for; matrix products, arithmetic and copies ran while one was open for 0% of the time, Pallas kernels for 4%

profile of v9, /device:TPU:1, one launch (start us, length us, event | category | flops | bytes accessed | tf_op | source)
XLA Modules:
  0.0 100.6 jit_solution(7287607849361180757)
XLA Ops:
  0.6 1.4 %select_convert_fusion = bf16[32,32,128]{2,1,0:T(8,128)(2,1)} fusion(f32[32,128]{1,0:T(8,128)} %bitcast.30), kind=kLoop, calls=%fused_computation | loop fusion | flops 524288 | bytes 278528 | tf_op jit(solution)/shard_map/convert_element_type | solution.py:303
  2.1 9.9 %all-to-all-start = ((bf16[32,32,128]{2,1,0:T(8,128)(2,1)}), bf16[32,32,128]{2,1,0:T(8,128)(2,1)S(1)}, u32[]{:S(2)}, u32[]{:S(2)}) async-start(bf16[32,32,128]{2,1,0:T(8,128)(2,1)} %select_convert_fusion), calls=%async_computation | async-start | bytes 524288 | tf_op jit(solution)/shard_map/all_to_all | solution.py:292
  12.0 3.9 %shard_map.112 = (bf16[22,256,256]{2,1,0:T(8,128)(2,1)S(1)}, f32[256,128]{1,0:T(8,128)S(1)}, f32[128,128]{1,0:T(8,128)S(1)}, f32[256,128]{1,0:T(8,128)S(1)}) custom-call(s32[64,256,128]{2,1,0:T(8,128)} %m_hbm.3, s32[1,64]{1,0:T(1,128)} %bitcast.41, s32[1,128]{1,0:T(1,128)} %bitcast.42, f32[16,256]{1,0:T(8,128)} %gain_hbm.1), custom_call_target="tpu_custom_call" | custom-call | flops 20971520 | bytes 12582912 | tf_op jit(solution)/shard_map/pallas_call | solution.py:34
  15.8 0.2 all-to-all-done.ag_ref
  16.0 0.0 copy-start.3
  16.0 0.0 copy-start.4
  16.0 2.1 %shard_map.113 = (f32[128,128]{1,0:T(8,128)S(1)}, bf16[10,256,256]{2,1,0:T(8,128)(2,1)S(1)}) custom-call(bf16[32,32,128]{2,1,0:T(8,128)(2,1)S(1)} %all-to-all-done.ag_ref, f32[256,128]{1,0:T(8,128)S(1)} %get-tuple-element.22.map_ref, f32[128,128]{1,0:T(8,128)S(1)} %get-tuple-element.23.note_ref, f32[256,128]{1,0:T(8,128)S(1)} %get-tuple-element.24.half_gain, ...), custom_call_target="tpu_custom_call" | custom-call | tf_op jit(solution)/shard_map/pallas_call | solution.py:34
  18.2 0.0 copy-start
  18.2 0.0 copy-start.1
  18.2 0.0 copy-start.2
  18.2 10.3 %all_to_all.40 = f32[32,4,128]{2,1,0:T(4,128)S(1)} all-to-all(f32[32,4,128]{2,1,0:T(4,128)S(1)} %bitcast.35), channel_id=1, replica_groups={{168,160,184,176,248,240,232,224,216,208,200,192,8,0,24,16,40,32,56,48,..., dimensions={0} | all-to-all | bytes 131072 | tf_op jit(solution)/shard_map/all_to_all | solution.py:292
  28.5 0.0 copy-done.3
  28.5 0.0 copy-done.4
  28.5 1.2 %shard_map.114 = (f32[256,128]{1,0:T(8,128)S(1)}, f32[1,128]{1,0:T(1,128)S(1)}, f32[1,128]{1,0:T(1,128)S(1)}) custom-call(f32[128,128]{1,0:T(8,128)S(1)} %bitcast.22, f32[1,128]{1,0:T(1,128)S(1)} %bitcast.38, f32[1,128]{1,0:T(1,128)S(1)} %bitcast.40, bf16[22,256,256]{2,1,0:T(8,128)(2,1)S(1)} %get-tuple-element.25.near_ref, ...), custom_call_target="tpu_custom_call" | custom-call | tf_op jit(solution)/shard_map/pallas_call | solution.py:34
  29.7 10.7 %all_to_all.41 = f32[32,8,128]{2,1,0:T(8,128)S(1)} all-to-all(f32[32,8,128]{2,1,0:T(8,128)S(1)} %bitcast.27), channel_id=1, replica_groups={{168,160,184,176,248,240,232,224,216,208,200,192,8,0,24,16,40,32,56,48,..., dimensions={0} | all-to-all | bytes 262144 | tf_op jit(solution)/shard_map/all_to_all | solution.py:292
  40.4 0.4 shard_map.115
  40.8 14.4 %all_to_all.42.in_ref = f32[8,64,128]{2,1,0:T(8,128)S(1)} all-to-all(f32[8,64,128]{2,1,0:T(8,128)S(1)} %get-tuple-element.29), channel_id=1, replica_groups={{6,4,0,2,5,7,1,3},{14,12,8,10,13,15,9,11},{22,20,16,18,21,23,17,19},{30..., dimensions={0} | all-to-all | bytes 524288 | tf_op jit(solution)/shard_map/all_to_all | solution.py:295
  55.2 0.0 copy-done
  55.2 0.0 copy-done.1
  55.2 0.0 copy-done.2
  55.2 0.1 shard_map.116
  55.3 11.7 %all_to_all.43 = bf16[32,4,128]{2,1,0:T(4,128)(2,1)S(1)} all-to-all(bf16[32,4,128]{2,1,0:T(4,128)(2,1)S(1)} %bitcast.36), channel_id=1, replica_groups={{168,160,184,176,248,240,232,224,216,208,200,192,8,0,24,16,40,32,56,48,..., dimensions={0} | all-to-all | bytes 65536 | tf_op jit(solution)/shard_map/all_to_all | solution.py:292
  67.0 0.7 shard_map.117
  67.7 10.0 %all_to_all.44 = f32[32,1,128]{2,1,0:T(1,128)S(1)} all-to-all(f32[32,1,128]{2,1,0:T(1,128)S(1)} %bitcast.29), channel_id=1, replica_groups={{168,160,184,176,248,240,232,224,216,208,200,192,8,0,24,16,40,32,56,48,..., dimensions={0} | all-to-all | bytes 32768 | tf_op jit(solution)/shard_map/all_to_all | solution.py:292
  77.7 1.2 %shard_map.118 = (f32[128,128]{1,0:T(8,128)S(1)}, f32[1,128]{1,0:T(1,128)}) custom-call(f32[32,128]{1,0:T(8,128)S(1)} %bitcast.28, f32[1,128]{1,0:T(1,128)S(1)} %bitcast.39, f32[1,128]{1,0:T(1,128)S(1)} %get-tuple-element.32.site_ref, f32[1,128]{1,0:T(1,128)S(1)} %get-tuple-element.33.sum_ref, bf16[22,256,256]{2,1,0:T(8,128)(2,1)S(1)} %get-tuple-element.25.near_ref, ...), custom_call_target="tpu_custom_call" | custom-call | tf_op jit(solution)/shard_map/pallas_call | solution.py:34
  78.9 10.7 %all_to_all.45 = f32[32,4,128]{2,1,0:T(4,128)S(1)} all-to-all(f32[32,4,128]{2,1,0:T(4,128)S(1)} %bitcast.34), channel_id=1, replica_groups={{168,160,184,176,248,240,232,224,216,208,200,192,8,0,24,16,40,32,56,48,..., dimensions={0} | all-to-all | bytes 131072 | tf_op jit(solution)/shard_map/all_to_all | solution.py:292
  89.6 0.2 shard_map.119
  89.8 10.2 %all_to_all.46.in_ref = f32[8,32,128]{2,1,0:T(8,128)S(1)} all-to-all(f32[8,32,128]{2,1,0:T(8,128)S(1)} %shard_map.119), channel_id=1, replica_groups={{6,4,0,2,5,7,1,3},{14,12,8,10,13,15,9,11},{22,20,16,18,21,23,17,19},{30..., dimensions={0} | all-to-all | bytes 262144 | tf_op jit(solution)/shard_map/all_to_all | solution.py:295
  99.9 0.6 shard_map.120
Async XLA Ops:
  2.1 14.0 %all-to-all-start = ((bf16[32,32,128]{2,1,0:T(8,128)(2,1)}), bf16[32,32,128]{2,1,0:T(8,128)(2,1)S(1)}, u32[]{:S(2)}, u32[]{:S(2)}) async-start(bf16[32,32,128]{2,1,0:T(8,128)(2,1)} %select_convert_fusion), calls=%async_computation | async-start | bytes 524288 | tf_op jit(solution)/shard_map/all_to_all | solution.py:292
  16.0 12.5 %copy-start.3 = (f32[128]{0:T(128)S(1)}, f32[128]{0:T(128)}, u32[]{:S(2)}) copy-start(f32[128]{0:T(128)} %param.13) | copy-start | bytes 1540
  16.0 12.5 %copy-start.4 = (f32[128]{0:T(128)S(1)}, f32[128]{0:T(128)}, u32[]{:S(2)}) copy-start(f32[128]{0:T(128)} %param.15) | copy-start | bytes 1540
  18.2 37.0 %copy-start = (f32[4096]{0:T(1024)S(1)}, f32[4096]{0:T(1024)}, u32[]{:S(2)}) copy-start(f32[4096]{0:T(1024)} %param.17) | copy-start | bytes 49156
  18.2 37.0 %copy-start.1 = (f32[4096]{0:T(1024)S(1)}, f32[4096]{0:T(1024)}, u32[]{:S(2)}) copy-start(f32[4096]{0:T(1024)} %param.14) | copy-start | bytes 49156
  18.2 37.0 %copy-start.2 = (f32[4096]{0:T(1024)S(1)}, f32[4096]{0:T(1024)}, u32[]{:S(2)}) copy-start(f32[4096]{0:T(1024)} %param.16) | copy-start | bytes 49156
